TPU v7x, 1024 devices: a whole 4x4x32 slice. The times are simulated.
1024 devices in a mesh: dom: 16 (over x_hi, y, core), fsdp: 64 (over z, x_lo).
Axes of the slice: x: 4 (x_hi: 2, x_lo: 2; x = x_hi * 2 + x_lo), y: 4, z: 32, core: 2. Of those that a mesh axis runs over, the one named last changes fastest.
Arguments:
- tokens: bfloat16 [262144, 1536], P(('dom', 'fsdp')), may hold values from -24 to 24
- gain: bfloat16 [1536], P('fsdp'), may hold values from 0.099609375 to 1.8984375
- kv_weight: bfloat16 [1536, 512], P('fsdp'), may hold values from -0.15625 to 0.15625
- positions: int32 [262144], P(('dom', 'fsdp')), may hold values from 0 to 4095
- cotangent: bfloat16 [262144, 512], P(('dom', 'fsdp')), may hold values from -6 to 6
- counts: int32 [16, 64], replicated, may hold values from 0 to 2, as said below
- ratios: int32 [16], replicated, may hold values from 1 to 8
Outputs:
- keys_values: bfloat16 [262144, 512], P(('dom', 'fsdp'))
- weight_grad: float32 [1536, 512], P('fsdp')
- gain_grad: float32 [1536], P('fsdp')
Inputs may be any that keep to these rules, and one draw needn't show every extreme that they name: counts gives each device's live rows in blocks of 128; every domain has a device with one or more live blocks, and some device holds 2 live blocks in every draw.
All inputs are finite; a program needn't handle non-finite values.
Results may differ from a plain program's by a relative error of at most 0.0051.
Values may be sent and summed in bfloat16 or wider, within the bound.
A program may use at most 32 MiB of HBM per device.

v0:
```python
import jax
import jax.numpy as jnp
from jax import lax
from jax.sharding import PartitionSpec as P

KVH = 2
HD = 128
BLOCK = 128


def rotary_tables(position_ids, half_width, head_size):
    exponents = jnp.arange(half_width, dtype=jnp.float32) * (2.0 / head_size)
    frequency = jnp.power(jnp.float32(1000000.0), -exponents)
    angles = position_ids.astype(jnp.float32)[:, None] * frequency[None, :]
    return (jnp.cos(angles)[:, None, :], jnp.sin(angles)[:, None, :])


def rotate_heads(values, cosines, sines, heads, head_size, direction):
    rows = values.shape[0]
    half_width = head_size // 2
    shaped = values.reshape(rows, heads, head_size)
    first = shaped[:, :, :half_width]
    second = shaped[:, :, half_width:]
    turned = jnp.concatenate(
        [
            first * cosines - direction * second * sines,
            second * cosines + direction * first * sines,
        ],
        axis=2,
    )
    return turned.reshape(rows, heads * head_size)


def backward_terms(scaled, normed, upstream, weights):
    weight_term = lax.dot_general(
        scaled, upstream, (((0,), (0,)), ((), ())), preferred_element_type=jnp.float32
    )
    scaled_grad = lax.dot_general(
        upstream, weights, (((1,), (1,)), ((), ())), preferred_element_type=jnp.float32
    )
    gain_term = jnp.sum(scaled_grad * normed, axis=0)
    return (weight_term, gain_term)


def body(tokens, gain, kv_weight, positions, cotangent, counts, ratios):
    domain_index = lax.axis_index("dom")
    member = lax.axis_index("fsdp")
    weights, gains = (
        lax.all_gather(kv_weight, "fsdp", axis=0, tiled=True),
        lax.all_gather(gain, "fsdp", axis=0, tiled=True),
    )
    row_count = tokens.shape[0]
    key_width = KVH * HD
    token_float = tokens.astype(jnp.float32)
    mean_square = jnp.mean(token_float * token_float, axis=1, keepdims=True)
    normed = token_float * lax.rsqrt(mean_square + 1e-06)
    scaled = (normed * gains.astype(jnp.float32)[None, :]).astype(jnp.bfloat16)
    projected = jnp.dot(scaled, weights, preferred_element_type=jnp.float32)
    cosines, sines = rotary_tables(positions, HD // 2, HD)
    keys_out = jnp.concatenate(
        [
            rotate_heads(projected[:, :key_width], cosines, sines, KVH, HD, 1.0),
            projected[:, key_width:],
        ],
        axis=1,
    ).astype(jnp.bfloat16)
    domain_rows = (BLOCK * jnp.sum(counts, axis=1)).astype(jnp.float32)
    live_total = jnp.sum(domain_rows)
    ratio_float = ratios.astype(jnp.float32)
    factor = ratio_float / jnp.sum(ratio_float) * live_total / domain_rows
    domain_hits = jnp.arange(counts.shape[0]) == domain_index
    own_factor = jnp.sum(jnp.where(domain_hits, factor, jnp.float32(0.0)))
    member_hits = domain_hits[:, None] & (jnp.arange(counts.shape[1]) == member)[None, :]
    own_blocks = jnp.sum(jnp.where(member_hits, counts, 0))
    live_rows = jnp.arange(row_count, dtype=jnp.int32) < BLOCK * own_blocks
    row_factor = jnp.where(live_rows, own_factor, jnp.float32(0.0))
    weighted = cotangent.astype(jnp.float32) * row_factor[:, None]
    upstream = jnp.concatenate(
        [
            rotate_heads(weighted[:, :key_width], cosines, sines, KVH, HD, -1.0),
            weighted[:, key_width:],
        ],
        axis=1,
    ).astype(jnp.bfloat16)
    weight_term, gain_term = backward_terms(scaled, normed, upstream, weights)
    share_w, share_g = (
        lax.psum_scatter(weight_term, "fsdp", scatter_dimension=0, tiled=True),
        lax.psum_scatter(gain_term, "fsdp", scatter_dimension=0, tiled=True),
    )
    weight_sum, gain_sum = lax.psum((share_w, share_g), "dom")
    root = jnp.sqrt(live_total)
    return (keys_out, weight_sum / root, gain_sum / root)


def solution(mesh):
    return jax.shard_map(
        body,
        mesh=mesh,
        in_specs=(
            P(("dom", "fsdp"), None),
            P("fsdp"),
            P("fsdp", None),
            P(("dom", "fsdp")),
            P(("dom", "fsdp"), None),
            P(),
            P(),
        ),
        out_specs=(P(("dom", "fsdp"), None), P("fsdp", None), P("fsdp")),
        check_vma=False,
    )
```

profile of v0, /device:TPU:1, one launch (start us, length us, event | category | flops | bytes accessed | tf_op | source)
XLA Modules:
  0.0 617.8 jit_solution(18254877547944198317)
XLA Ops:
  7.2 0.7 all-gather.2.cloned.1.call-update
  8.0 1.4 select_reduce_fusion
  10.1 1.3 convert_reduce_fusion
  11.4 2.6 select_reduce_fusion.1
  13.9 0.6 compare_select_fusion
  14.6 1.1 convert_multiply_fusion.2
  15.7 1.4 fusion.10
  17.7 0.2 dynamic-update-slice
  18.0 111.2 %all-reduce = bf16[1536]{0:T(1024)(128)(2,1)S(1)} all-reduce(bf16[1536]{0:T(1024)(128)(2,1)S(1)} %dynamic-update-slice), channel_id=1, replica_groups=mesh['dom'=16,'fsdp'=64] {'fsdp'}, use_global_device_ids=true, to_apply=%add | all-reduce | flops 1536 | bytes 6144
  129.4 0.2 fusion.2
  129.6 0.5 broadcast_multiply_fusion
  130.2 103.3 %all-gather.2.cloned.1.call-done = bf16[1536,512]{1,0:T(8,128)(2,1)} async-done(((bf16[24,512]{1,0:T(8,128)(2,1)}), bf16[1536,512]{1,0:T(8,128)(2,1)}) %all-gather.2.cloned.1.call-update) | async-done | bytes 1572880 | tf_op jit(solution)/shard_map/all_gather | solution.py:49
  233.5 2.0 fusion.6
  235.7 0.8 subtract_convert_fusion
  236.5 0.4 pad_maximum_fusion.5
  236.9 2.4 fusion.4
  240.8 0.4 pad_maximum_fusion.4
  241.2 0.6 fusion.3
  241.8 97.9 %all-reduce.1 = f32[1536]{0:T(1024)S(1)} all-reduce(f32[1536]{0:T(1024)S(1)} %fusion.3), channel_id=3, replica_groups=mesh['dom'=16,'fsdp'=64] {'fsdp'}, use_global_device_ids=true, to_apply=%region_9.10.clone | all-reduce | flops 1536 | bytes 12288
  339.8 0.7 pad_maximum_fusion
  340.5 160.6 %reduce-scatter.2.cloned.1.call-done = f32[24,512]{1,0:T(8,128)} async-done(((f32[1536,512]{1,0:T(8,128)}), f32[24,512]{1,0:T(8,128)}) %reduce-scatter.2.cloned.1.call-update) | async-done | bytes 49168 | tf_op jit(solution)/shard_map/reduce_scatter | solution.py:87
  501.1 108.8 %all-reduce.2 = (f32[24,512]{1,0:T(8,128)S(1)}, f32[24]{0:T(128)S(1)}) all-reduce(f32[24,512]{1,0:T(8,128)} %reduce-scatter.2.cloned.1.call-done, f32[24]{0:T(128)S(1)} %dynamic-slice.2), channel_id=1, replica_groups=mesh['dom'=16,'fsdp'=64] {'dom'}, use_global_device_ids=true, to_apply=%region_7.8 | all-reduce | flops 12312 | bytes 98496 | tf_op jit(solution)/shard_map/psum | solution.py:90
  609.8 0.6 broadcast_divide_fusion
  610.5 0.5 broadcast_divide_fusion.1
  (27 shorter events, 0.6 us)
Async XLA Ops:
  7.2 8.5 %copy-start.1 = (s32[256]{0:T(256)S(1)}, s32[256]{0:T(256)}, u32[]{:S(2)}) copy-start(s32[256]{0:T(256)} %param.10) | copy-start | bytes 3076
  7.2 10.6 %copy-start.3 = (bf16[24]{0:T(256)(128)(2,1)S(1)}, bf16[24]{0:T(256)(128)(2,1)}, u32[]{:S(2)}) copy-start(bf16[24]{0:T(256)(128)(2,1)} %param.8) | copy-start | bytes 148
  7.2 122.2 %copy-start = (bf16[256,1536]{1,0:T(8,128)(2,1)S(1)}, bf16[256,1536]{1,0:T(8,128)(2,1)}, u32[]{:S(2)}) copy-start(bf16[256,1536]{1,0:T(8,128)(2,1)} %param.7) | copy-start | bytes 2359300
  7.2 226.3 %all-gather.2.cloned.1.call-start = ((), (), s32[]{:S(2)}) async-start(), calls=%async_computation.1 | async-start | bytes 1597440 | tf_op jit(solution)/shard_map/all_gather | solution.py:49
  7.9 493.1 %reduce-scatter.2.cloned.1.call-start = ((), (), s32[]{:S(2)}) async-start(), calls=%async_computation.2 | async-start | bytes 3194880 | tf_op jit(solution)/shard_map/reduce_scatter | solution.py:87
  239.3 1.9 copy-start.2
Sparse Core Ops, SparseCore 0:
  10.7 222.7 all-gather.1
  239.5 261.5 reduce-scatter.1
where the time goes:
time: 622 us; the launch traced here: 618 us
  blocking collectives  318 us (51%)
  waiting for transfers between devices  265 us (43%)
  between operations  17 us (3%)
  other arithmetic  11.2 us (2%)
    unnamed x2, blocking collectives  209 us
    reduce_scatter x1, waiting for transfers between devices, body(): lax.psum_scatter(weight_term, 'fsdp', scatter_dimension=0, tiled=True)  161 us
    psum x1, blocking collectives, body(): weight_sum, gain_sum = lax.psum((share_w, share_g), 'dom')  109 us
    all_gather x1, waiting for transfers between devices, body(): lax.all_gather(kv_weight, 'fsdp', axis=0, tiled=True)  103 us
  transfers between devices with their start and end apart: 2, of which 2 were waited for; matrix products, arithmetic and copies ran while one was open for 2% of the time, Pallas kernels for 0%

commit v1 on v0

v1 whole, which is shorter than its diff:
```python
import functools

import jax
import jax.numpy as jnp
import numpy as np
from jax import lax
from jax.experimental import pallas as pl
from jax.experimental.pallas import tpu as pltpu
from jax.sharding import PartitionSpec as P

HD = 128
HALF = HD // 2
BLOCK = 128
LANES = 128
MESH = pl.DeviceIdType.MESH
F32 = jnp.float32
BF16 = jnp.bfloat16


def to_column(row, size):
    eye = lax.broadcasted_iota(jnp.int32, (size, size), 0) == lax.broadcasted_iota(
        jnp.int32, (size, size), 1
    )
    return jnp.sum(jnp.where(eye, row, jnp.float32(0.0)), axis=1, keepdims=True)


def to_row(column, size):
    eye = lax.broadcasted_iota(jnp.int32, (size, size), 0) == lax.broadcasted_iota(
        jnp.int32, (size, size), 1
    )
    return jnp.sum(jnp.where(eye, column, jnp.float32(0.0)), axis=0, keepdims=True)


def kernel(
    ny,
    nz,
    counts_ref,
    ratios_ref,
    gain_ref,
    weight_ref,
    positions_ref,
    freq_ref,
    tokens_ref,
    cot_ref,
    kv_ref,
    wg_ref,
    gg_ref,
    own_gw,
    land_g1,
    piece_g,
    full_gw,
    part_m,
    land_r0,
    sum_r0,
    land_r1,
    sum_r1,
    land_r2,
    sum_r2,
    land_r3,
    upstream,
    sem_g1s,
    sem_g1r,
    sem_g2s,
    sem_g2r,
    sem_g3s,
    sem_g3r,
    sem_r0s,
    sem_r0r,
    sem_r1s,
    sem_r1r,
    sem_r2s,
    sem_r2r,
    sem_r3s,
    sem_r3r,
):
    dom = lax.axis_index("dom")
    fsdp = lax.axis_index("fsdp")
    core = lax.rem(dom, 2)
    y = lax.rem(dom // 2, ny)
    x_hi = dom // (2 * ny)
    z = fsdp // 2
    x_lo = lax.rem(fsdp, 2)
    x = x_hi * 2 + x_lo
    q = x_hi * 2 + core
    jn = nz // 8
    rows = tokens_ref.shape[0]
    shard = weight_ref.shape[0]
    cols = weight_ref.shape[1]
    slab = 2 * shard
    key_width = cols // 2
    heads = key_width // HD
    width = tokens_ref.shape[1]
    group = 8 * slab
    lo_own = lax.rem(z + core, 2)
    lo_sib = 1 - lo_own

    def dev(xx, yy, cc, zz):
        return ((xx // 2 * ny + yy) * 2 + cc, zz * 2 + lax.rem(xx, 2))

    def lane_tile(i):
        return pl.ds(pl.multiple_of(i * LANES, LANES), LANES)

    barrier = pltpu.get_barrier_semaphore()

    def greet_plane(i, carry):
        xx = lax.rem(x + i // (2 * ny), 4)
        yy = lax.rem(y + lax.rem(i // 2, ny), ny)
        cc = lax.rem(core + lax.rem(i, 2), 2)
        pl.semaphore_signal(barrier, inc=1, device_id=dev(xx, yy, cc, z), device_id_type=MESH)
        return carry

    lax.fori_loop(1, 8 * ny, greet_plane, 0)

    steps = nz // 4

    def z_peers(s, sign):
        dist = q + 4 * s
        return lax.rem(z + sign * dist + 2 * nz, nz)

    def greet_z(i, carry):
        s, half = i // 2, lax.rem(i, 2)
        for sign in (1, -1):
            zz = z_peers(s, sign)

            @pl.when(zz != z)
            def _():
                pl.semaphore_signal(
                    barrier,
                    inc=1,
                    device_id=dev(x_hi * 2 + half, y, core, zz),
                    device_id_type=MESH,
                )

        return carry

    lax.fori_loop(0, 2 * steps, greet_z, 0)

    gain_col = to_column(gain_ref[...].astype(F32), shard)
    weight = weight_ref[...].astype(F32)
    own_gw[...] = (weight * gain_col).astype(BF16)

    n_self = jnp.where(lax.rem(q, 4) == 0, 4, 0)
    pl.semaphore_wait(barrier, 8 * ny - 1 + 4 * steps - n_self)

    def g1_copy(s):
        far = z_peers(s, 1)
        half = lax.rem(s, 2)
        return (
            far,
            half,
            pltpu.make_async_remote_copy(
                src_ref=own_gw.at[:, lane_tile(y)],
                dst_ref=land_g1.at[s // 2, x_lo],
                send_sem=sem_g1s.at[s],
                recv_sem=sem_g1r.at[s // 2, x_lo],
                device_id=dev(x_hi * 2 + half, y, core, far),
                device_id_type=MESH,
            ),
        )

    def g1_local():
        return pltpu.make_async_copy(
            own_gw.at[:, lane_tile(y)], land_g1.at[0, x_lo], sem_g1r.at[0, x_lo]
        )

    def is_self(far, half):
        return (far == z) & (half == x_lo)

    def g1_start(s, carry):
        far, half, copy = g1_copy(s)

        @pl.when(jnp.logical_not(is_self(far, half)))
        def _():
            copy.start()

        @pl.when(is_self(far, half))
        def _():
            g1_local().start()

        return carry

    lax.fori_loop(0, steps, g1_start, 0)

    counts = counts_ref[...].astype(F32)
    n_dom, n_mem = counts.shape
    domain_rows = BLOCK * jnp.sum(counts, axis=1, keepdims=True)
    live_total = jnp.sum(domain_rows, axis=0, keepdims=True)
    ratio = to_column(ratios_ref[...].astype(F32), n_dom)
    factor = ratio / jnp.sum(ratio, axis=0, keepdims=True) * live_total / domain_rows
    dom_ids = lax.broadcasted_iota(jnp.int32, (n_dom, 1), 0)
    own_factor = jnp.sum(jnp.where(dom_ids == dom, factor, 0.0), axis=0, keepdims=True)
    at_dom = lax.broadcasted_iota(jnp.int32, (n_dom, n_mem), 0) == dom
    at_mem = lax.broadcasted_iota(jnp.int32, (n_dom, n_mem), 1) == fsdp
    own_count = jnp.sum(
        jnp.sum(jnp.where(at_dom & at_mem, counts, 0.0), axis=1, keepdims=True),
        axis=0,
        keepdims=True,
    )
    row_ids = lax.broadcasted_iota(jnp.int32, (rows, 1), 0).astype(F32)
    row_factor = jnp.where(row_ids < BLOCK * own_count, own_factor, 0.0)

    token = tokens_ref[...].astype(F32)
    mean_square = jnp.sum(token * token, axis=1, keepdims=True) * (1.0 / width)
    inv_norm = lax.rsqrt(mean_square + 1e-06)

    pos = positions_ref[...].astype(F32)
    pos_col = jnp.concatenate(
        [to_column(pos[i : i + 1, :], LANES) for i in range(rows // LANES)], axis=0
    )
    angles = pos_col * freq_ref[...]
    cosines = jnp.cos(angles)
    lane_ids = lax.broadcasted_iota(jnp.int32, (rows, HD), 1)
    sines = jnp.where(lane_ids < HALF, -1.0, 1.0) * jnp.sin(angles)

    scale = row_factor * inv_norm
    for h in range(2 * heads):
        part = cot_ref[:, h * HD : (h + 1) * HD].astype(F32) * scale
        if h < heads:
            part = part * cosines - pltpu.roll(part, HALF, 1) * sines
        upstream[:, h * HD : (h + 1) * HD] = part.astype(BF16)

    def m_step(j, carry):
        lhs = tokens_ref[:, pl.ds(pl.multiple_of(j * group, group), group)]
        prod = lax.dot_general(
            lhs, upstream[...], (((0,), (0,)), ((), ())), preferred_element_type=F32
        )
        part_m[j] = prod.reshape(4, 2, slab, cols).astype(BF16)
        return carry

    lax.fori_loop(0, jn, m_step, 0)

    sibling = dev(x, y, 1 - core, z)
    r0 = pltpu.make_async_remote_copy(
        src_ref=part_m.at[:, :, lo_sib],
        dst_ref=land_r0,
        send_sem=sem_r0s,
        recv_sem=sem_r0r,
        device_id=sibling,
        device_id_type=MESH,
    )
    r0.start()

    own_class = q + 4 * x_lo
    r_gather = lax.rem(z - own_class + 2 * nz, 8)

    def g1_arrive(j, carry):
        for half in range(2):
            pltpu.make_async_copy(
                land_g1.at[j, half], land_g1.at[j, half], sem_g1r.at[j, half]
            ).wait()
        at = lax.rem(z - own_class - 8 * j + 2 * nz, nz) // 8
        both = jnp.concatenate(
            [land_g1[j, 0].astype(F32), land_g1[j, 1].astype(F32)], axis=0
        )
        piece_g[at] = both.astype(BF16)
        return carry

    lax.fori_loop(0, jn, g1_arrive, 0)

    r0.wait_recv()

    def r0_sum(i, carry):
        j, hi = i // 4, lax.rem(i, 4)
        total = part_m[j, hi, lo_own].astype(F32) + land_r0[j, hi].astype(F32)
        sum_r0[j, hi] = total.astype(BF16)
        return carry

    lax.fori_loop(0, 4 * jn, r0_sum, 0)

    def r1_copy(k):
        xx = lax.rem(x + k // ny, 4)
        yy = lax.rem(y + lax.rem(k, ny), ny)
        to_class = (xx // 2) * 2 + core + 4 * lax.rem(xx, 2)
        hi = lax.rem(z + to_class, 8) // 2
        return pltpu.make_async_remote_copy(
            src_ref=sum_r0.at[:, hi, :, lane_tile(yy)],
            dst_ref=land_r1.at[k],
            send_sem=sem_r1s.at[k],
            recv_sem=sem_r1r.at[k],
            device_id=dev(xx, yy, core, z),
            device_id_type=MESH,
        )

    def r1_start(k, carry):
        r1_copy(k).start()
        return carry

    lax.fori_loop(1, 4 * ny, r1_start, 0)

    hi_gather = r_gather // 2

    def g2_copy(k):
        xx = lax.rem(x + k // ny, 4)
        yy = lax.rem(y + lax.rem(k, ny), ny)
        return pltpu.make_async_remote_copy(
            src_ref=piece_g,
            dst_ref=full_gw.at[:, hi_gather, lo_own, :, lane_tile(y)],
            send_sem=sem_g2s.at[k],
            recv_sem=sem_g2r.at[k],
            device_id=dev(xx, yy, core, z),
            device_id_type=MESH,
        )

    g2_local = pltpu.make_async_copy(
        piece_g, full_gw.at[:, hi_gather, lo_own, :, lane_tile(y)], sem_g2r.at[0]
    )
    g2_local.start()

    def g2_start(k, carry):
        g2_copy(k).start()
        return carry

    lax.fori_loop(1, 4 * ny, g2_start, 0)

    hi_reduce = lax.rem(z + own_class, 8) // 2
    total1 = sum_r0[:, hi_reduce, :, lane_tile(y)].astype(F32)

    def r1_arrive(k, total):
        r1_copy(k).wait_recv()
        return total + land_r1[k].astype(F32)

    total1 = lax.fori_loop(1, 4 * ny, r1_arrive, total1)
    for half in range(2):
        sum_r1[:, half] = total1[:, half * shard : (half + 1) * shard, :].astype(BF16)

    def r2_copy(i):
        j, half = i // 2, lax.rem(i, 2)
        s = 2 * j + x_lo
        far = z_peers(s, 1)
        return (
            far,
            half,
            s,
            pltpu.make_async_remote_copy(
                src_ref=sum_r1.at[far // 8, half],
                dst_ref=land_r2.at[s],
                send_sem=sem_r2s.at[i],
                recv_sem=sem_r2r.at[s],
                device_id=dev(x_hi * 2 + half, y, core, far),
                device_id_type=MESH,
            ),
        )

    def r2_local():
        return pltpu.make_async_copy(
            sum_r1.at[z // 8, x_lo], land_r2.at[0], sem_r2r.at[0]
        )

    def r2_start(i, carry):
        far, half, s, copy = r2_copy(i)

        @pl.when(jnp.logical_not(is_self(far, half)))
        def _():
            copy.start()

        @pl.when(is_self(far, half))
        def _():
            r2_local().start()

        return carry

    lax.fori_loop(0, steps, r2_start, 0)

    g2_local.wait()

    def g2_arrive(k, carry):
        g2_copy(k).wait_recv()
        return carry

    lax.fori_loop(1, 4 * ny, g2_arrive, 0)
    g3 = pltpu.make_async_remote_copy(
        src_ref=full_gw.at[:, :, lo_own],
        dst_ref=full_gw.at[:, :, lo_own],
        send_sem=sem_g3s,
        recv_sem=sem_g3r,
        device_id=sibling,
        device_id_type=MESH,
    )
    g3.start()

    def r2_arrive(s, total):
        pltpu.make_async_copy(land_r2.at[s], land_r2.at[s], sem_r2r.at[s]).wait()
        return total + land_r2[s].astype(F32)

    sum_r2[...] = lax.fori_loop(
        0, steps, r2_arrive, jnp.zeros((shard, LANES), F32)
    )

    def r3_copy(i):
        hh = lax.rem(x_hi + i // (2 * ny), 2)
        yy = lax.rem(y + lax.rem(i // 2, ny), ny)
        cc = lax.rem(core + lax.rem(i, 2), 2)
        return pltpu.make_async_remote_copy(
            src_ref=sum_r2,
            dst_ref=land_r3.at[q, :, lane_tile(y)],
            send_sem=sem_r3s.at[i],
            recv_sem=sem_r3r.at[i],
            device_id=dev(hh * 2 + x_lo, yy, cc, z),
            device_id_type=MESH,
        )

    r3_local = pltpu.make_async_copy(
        sum_r2, land_r3.at[q, :, lane_tile(y)], sem_r3r.at[0]
    )
    r3_local.start()

    def r3_start(i, carry):
        r3_copy(i).start()
        return carry

    lax.fori_loop(1, 4 * ny, r3_start, 0)

    pltpu.make_async_remote_copy(
        src_ref=full_gw.at[:, :, lo_sib],
        dst_ref=full_gw.at[:, :, lo_sib],
        send_sem=sem_g3s,
        recv_sem=sem_g3r,
        device_id=sibling,
        device_id_type=MESH,
    ).wait_recv()

    def p_step(j, total):
        lhs = tokens_ref[:, pl.ds(pl.multiple_of(j * group, group), group)]
        rhs = full_gw[j].reshape(group, cols)
        return total + jnp.dot(lhs, rhs, preferred_element_type=F32)

    projected = lax.fori_loop(0, jn, p_step, jnp.zeros((rows, cols), F32))
    projected = projected * inv_norm
    for h in range(2 * heads):
        part = projected[:, h * HD : (h + 1) * HD]
        if h < heads:
            part = part * cosines + pltpu.roll(part, HALF, 1) * sines
        kv_ref[:, h * HD : (h + 1) * HD] = part.astype(BF16)

    r3_local.wait()

    def r3_arrive(i, carry):
        r3_copy(i).wait_recv()
        return carry

    lax.fori_loop(1, 4 * ny, r3_arrive, 0)
    total = land_r3[0] + land_r3[1] + land_r3[2] + land_r3[3]
    root = jnp.sqrt(live_total)
    wg_ref[...] = total * gain_col / root
    gain_sum = jnp.sum(total * weight, axis=1, keepdims=True)
    gg_ref[...] = to_row(gain_sum / root, shard)

    def g1_drain(s, carry):
        far, half, copy = g1_copy(s)

        @pl.when(jnp.logical_not(is_self(far, half)))
        def _():
            copy.wait_send()

        return carry

    def r2_drain(i, carry):
        far, half, s, copy = r2_copy(i)

        @pl.when(jnp.logical_not(is_self(far, half)))
        def _():
            copy.wait_send()

        return carry

    def drain(k, carry):
        r1_copy(k).wait_send()
        g2_copy(k).wait_send()
        r3_copy(k).wait_send()
        return carry

    lax.fori_loop(0, steps, g1_drain, 0)
    lax.fori_loop(0, steps, r2_drain, 0)
    lax.fori_loop(1, 4 * ny, drain, 0)
    r0.wait_send()
    g3.wait_send()


def body(ny, nz, tokens, gain, kv_weight, positions, cotangent, counts, ratios):
    rows, width = tokens.shape
    shard, cols = kv_weight.shape
    jn, steps, plane = nz // 8, nz // 4, 4 * ny
    slab = 2 * shard
    exponents = np.arange(HALF) * (2.0 / HD)
    freq = np.power(1000000.0, -exponents).astype(np.float32)
    freq = jnp.asarray(np.concatenate([freq, freq])[None, :])
    vmem = pl.BlockSpec(memory_space=pltpu.VMEM)
    dma = pltpu.SemaphoreType.DMA
    kv, wg, gg = pl.pallas_call(
        functools.partial(kernel, ny, nz),
        out_shape=(
            jax.ShapeDtypeStruct((rows, cols), BF16),
            jax.ShapeDtypeStruct((shard, cols), F32),
            jax.ShapeDtypeStruct((1, shard), F32),
        ),
        in_specs=[vmem] * 8,
        out_specs=(vmem, vmem, vmem),
        scratch_shapes=[
            pltpu.VMEM((shard, cols), BF16),
            pltpu.VMEM((jn, 2, shard, LANES), BF16),
            pltpu.VMEM((jn, slab, LANES), BF16),
            pltpu.VMEM((jn, 4, 2, slab, cols), BF16),
            pltpu.VMEM((jn, 4, 2, slab, cols), BF16),
            pltpu.VMEM((jn, 4, slab, cols), BF16),
            pltpu.VMEM((jn, 4, slab, cols), BF16),
            pltpu.VMEM((plane, jn, slab, LANES), BF16),
            pltpu.VMEM((jn, 2, shard, LANES), BF16),
            pltpu.VMEM((steps, shard, LANES), BF16),
            pltpu.VMEM((shard, LANES), F32),
            pltpu.VMEM((4, shard, cols), F32),
            pltpu.VMEM((rows, cols), BF16),
            dma((steps,)),
            dma((jn, 2)),
            dma((plane,)),
            dma((plane,)),
            dma,
            dma,
            dma,
            dma,
            dma((plane,)),
            dma((plane,)),
            dma((steps,)),
            dma((steps,)),
            dma((plane,)),
            dma((plane,)),
        ],
        compiler_params=pltpu.CompilerParams(
            collective_id=0, has_side_effects=True, vmem_limit_bytes=40 * 2**20
        ),
        name="kv_exchange",
    )(
        counts,
        ratios.reshape(1, -1),
        gain.reshape(1, -1),
        kv_weight,
        positions.reshape(-1, LANES),
        freq,
        tokens,
        cotangent,
    )
    return (kv, wg, gg.reshape(-1))


def solution(mesh):
    ny = mesh.shape["dom"] // 4
    nz = mesh.shape["fsdp"] // 2
    return jax.shard_map(
        functools.partial(body, ny, nz),
        mesh=mesh,
        in_specs=(
            P(("dom", "fsdp"), None),
            P("fsdp"),
            P("fsdp", None),
            P(("dom", "fsdp")),
            P(("dom", "fsdp"), None),
            P(),
            P(),
        ),
        out_specs=(P(("dom", "fsdp"), None), P("fsdp", None), P("fsdp")),
        check_vma=False,
    )
```

time: 622 us -> 85.4 us (0.14)
  blocking collectives: 318 us -> 0 us
  waiting for transfers between devices: 265 us -> 0 us
  Pallas kernels: 0 us -> 78.3 us
  between operations: 17 us -> 0.68 us
  other arithmetic: 11.2 us -> 0 us
    unnamed x2 -> x0, blocking collectives: 209 us -> none
    reduce_scatter x1 -> x0, waiting for transfers between devices: 161 us -> none  [body(): lax.psum_scatter(weight_term, 'fsdp', scatter_dimension=0, tiled=True)]
    psum x1 -> x0, blocking collectives: 109 us -> none  [body(): weight_sum, gain_sum = lax.psum((share_w, share_g), 'dom')]
    all_gather x1 -> x0, waiting for transfers between devices: 103 us -> none  [body(): lax.all_gather(kv_weight, 'fsdp', axis=0, tiled=True)]
    pallas_call x0 -> x1, Pallas kernels: none -> 78.3 us  [body(): pl.pallas_call(functools.partial(kernel, ny, nz), out_shape=(jax.ShapeDty...]
  transfers between devices with their start and end apart: 2 -> 0, of which waited for: 2 -> 0; matrix products, arithmetic and copies ran while one was open for 2% -> 0% of each run, Pallas kernels for 0% -> 0%
where the time goes in v1:
time: 85.4 us; the launch traced here: 85 us
  Pallas kernels  78.3 us (92%)
  local copies, waits for them, and re-layouts  6.03 us (7%)
    pallas_call x1, Pallas kernels, body(): pl.pallas_call(functools.partial(kernel, ny, nz), out_shape=(jax.ShapeDty...  78.3 us
    unnamed x19, local copies, waits for them, and re-layouts  6.03 us

profile of v1, /device:TPU:1, one launch (start us, length us, event | category | flops | bytes accessed | tf_op | source)
XLA Modules:
  0.0 85.0 jit_solution(13276577740062160699)
XLA Ops:
  0.6 0.0 copy-start.6
  0.6 0.0 copy-start.7
  0.7 0.0 copy-start.4
  0.7 0.0 copy-start.5
  0.7 0.6 copy-done.6
  1.3 0.0 copy-done.7
  1.3 0.0 copy-done.4
  1.3 0.0 copy-done.5
  1.3 0.0 copy-start
  1.3 1.1 %copy-done = bf16[256,1536]{1,0:T(8,128)(2,1)S(1)} copy-done((bf16[256,1536]{1,0:T(8,128)(2,1)S(1)}, bf16[256,1536]{1,0:T(8,128)(2,1)}, u32[]{:S(2)}) %copy-start) | copy-done | bytes 786456
  2.5 0.0 copy-start.1
  2.5 0.9 %copy-done.1 = bf16[256,512]{1,0:T(8,128)(2,1)S(1)} copy-done((bf16[256,512]{1,0:T(8,128)(2,1)S(1)}, bf16[256,512]{1,0:T(8,128)(2,1)}, u32[]{:S(2)}) %copy-start.1) | copy-done | bytes 262168
  3.4 0.0 copy-start.2
  3.4 0.7 copy-done.2
  4.2 0.0 copy-start.3
  4.2 0.7 copy-done.3
  4.9 78.3 %kv_exchange.1 = (bf16[256,512]{1,0:T(8,128)(2,1)S(1)}, f32[24,512]{1,0:T(8,128)S(1)}, f32[1,24]{1,0:T(1,128)S(1)}) custom-call(s32[16,64]{1,0:T(8,128)S(1)} %copy-done.3, s32[1,16]{1,0:T(1,128)S(1)} %bitcast.5, bf16[1,24]{1,0:T(2,128)(2,1)S(1)} %bitcast.6, bf16[24,512]{1,0:T(8,128)(2,1)S(1)} %copy-done.2, s32[2,128]{1,0:T(2,128)S(1)} %bitcast.4, ...), custom_call_target="tpu_custom_call" | custom-call | tf_op jit(solution)/shard_map/kv_exchange/pallas_call | solution.py:489
  83.2 0.7 copy.14
  83.9 0.6 copy.15
  84.5 0.5 copy.16
Async XLA Ops:
  0.6 0.7 copy-start.6
  0.6 0.7 copy-start.7
  0.7 0.7 copy-start.4
  0.7 0.7 copy-start.5
  1.3 1.1 %copy-start = (bf16[256,1536]{1,0:T(8,128)(2,1)S(1)}, bf16[256,1536]{1,0:T(8,128)(2,1)}, u32[]{:S(2)}) copy-start(bf16[256,1536]{1,0:T(8,128)(2,1)} %tokens_ref.1) | copy-start | bytes 2359300
  2.5 0.9 %copy-start.1 = (bf16[256,512]{1,0:T(8,128)(2,1)S(1)}, bf16[256,512]{1,0:T(8,128)(2,1)}, u32[]{:S(2)}) copy-start(bf16[256,512]{1,0:T(8,128)(2,1)} %cot_ref.1) | copy-start | bytes 786436
  3.4 0.7 copy-start.2
  4.2 0.7 copy-start.3

commit v2 on v1

v2 whole, which is shorter than its diff:
```python
import functools

import jax
import jax.numpy as jnp
import numpy as np
from jax import lax
from jax.experimental import pallas as pl
from jax.experimental.pallas import tpu as pltpu
from jax.sharding import PartitionSpec as P

HD = 128
HALF = HD // 2
BLOCK = 128
LANES = 128
MESH = pl.DeviceIdType.MESH
F32 = jnp.float32
BF16 = jnp.bfloat16


def to_column(row, size):
    eye = lax.broadcasted_iota(jnp.int32, (size, size), 0) == lax.broadcasted_iota(
        jnp.int32, (size, size), 1
    )
    return jnp.sum(jnp.where(eye, row, jnp.float32(0.0)), axis=1, keepdims=True)


def to_row(column, size):
    eye = lax.broadcasted_iota(jnp.int32, (size, size), 0) == lax.broadcasted_iota(
        jnp.int32, (size, size), 1
    )
    return jnp.sum(jnp.where(eye, column, jnp.float32(0.0)), axis=0, keepdims=True)


def kernel(
    ny,
    nz,
    counts_hbm,
    ratios_hbm,
    gain_hbm,
    weight_hbm,
    positions_hbm,
    freq_hbm,
    tokens_hbm,
    cot_hbm,
    kv_ref,
    wg_ref,
    gg_ref,
    counts_ref,
    ratios_ref,
    gain_ref,
    weight_ref,
    positions_ref,
    freq_ref,
    tokens_ref,
    cot_ref,
    own_gw,
    land_g1,
    piece_g,
    full_gw,
    part_m,
    land_r0,
    sum_r0,
    land_r1,
    sum_r1,
    land_r2,
    sum_r2,
    land_r3,
    upstream,
    sem_in,
    sem_g1s,
    sem_g1r,
    sem_gxs,
    sem_gxr,
    sem_g2s,
    sem_g2r,
    sem_g3s,
    sem_g3r,
    sem_r0s,
    sem_r0r,
    sem_r1s,
    sem_r1r,
    sem_r2s,
    sem_r2r,
    sem_r3s,
    sem_r3r,
):
    dom = lax.axis_index("dom")
    fsdp = lax.axis_index("fsdp")
    core = lax.rem(dom, 2)
    y = lax.rem(dom // 2, ny)
    x_hi = dom // (2 * ny)
    z = fsdp // 2
    x_lo = lax.rem(fsdp, 2)
    x = x_hi * 2 + x_lo
    q = x_hi * 2 + core
    jn = nz // 8
    plane = 4 * ny
    steps = 2 * jn
    rows, width = tokens_ref.shape
    shard, cols = weight_ref.shape
    slab = 2 * shard
    key_width = cols // 2
    heads = key_width // HD
    group = 8 * slab
    lo_own = lax.rem(z + core, 2)
    lo_sib = 1 - lo_own

    def dev(xx, yy, cc, zz):
        return ((xx // 2 * ny + yy) * 2 + cc, zz * 2 + lax.rem(xx, 2))

    def remote(src, dst, send, recv, device):
        return pltpu.make_async_remote_copy(
            src_ref=src,
            dst_ref=dst,
            send_sem=send,
            recv_sem=recv,
            device_id=device,
            device_id_type=MESH,
        )

    def lane_tile(i):
        return pl.ds(pl.multiple_of(i * LANES, LANES), LANES)

    def wrap_z(value):
        return lax.rem(value + 2 * nz, nz)

    loads = [
        pltpu.make_async_copy(src, dst, sem_in.at[i])
        for i, (src, dst) in enumerate(
            (
                (tokens_hbm, tokens_ref),
                (cot_hbm, cot_ref),
                (positions_hbm, positions_ref),
                (freq_hbm, freq_ref),
                (weight_hbm, weight_ref),
                (gain_hbm, gain_ref),
                (counts_hbm, counts_ref),
                (ratios_hbm, ratios_ref),
            )
        )
    ]
    for load in loads:
        load.start()

    own_class = q + 4 * x_lo
    own_shift = q - 4 * x_lo
    residue = lax.rem(z - own_class + 2 * nz, 8)
    hi_own = residue // 2
    home = wrap_z(z - own_shift) // 8

    barrier = pltpu.get_barrier_semaphore()

    def greet(device):
        pl.semaphore_signal(barrier, inc=1, device_id=device, device_id_type=MESH)

    def greet_plane(i, carry):
        xx = lax.rem(x + i // (2 * ny), 4)
        yy = lax.rem(y + lax.rem(i // 2, ny), ny)
        cc = lax.rem(core + lax.rem(i, 2), 2)
        greet(dev(xx, yy, cc, z))
        return carry

    lax.fori_loop(1, 2 * plane, greet_plane, 0)
    near_self = (own_class == 0).astype(jnp.int32)
    for half in range(2):
        owner = dev(x_hi * 2 + half, y, core, wrap_z(z - own_shift))
        if half == 0:

            @pl.when(own_class != 0)
            def _(owner=owner):
                greet(owner)

        else:
            greet(owner)
    ring = min(jn - 1, 2)
    ahead = dev(x, y, core, wrap_z(z + 8))
    behind = dev(x, y, core, wrap_z(z - 8))
    if jn > 1:
        greet(ahead)
    if jn > 2:
        greet(behind)

    loads[4].wait()
    loads[5].wait()
    gain_col = to_column(gain_ref[...].astype(F32), shard)
    weight = weight_ref[...].astype(F32)
    own_gw[...] = (weight * gain_col).astype(BF16)

    loads[2].wait()
    loads[3].wait()
    pos = positions_ref[...].astype(F32)
    pos_col = jnp.concatenate(
        [to_column(pos[i : i + 1, :], LANES) for i in range(rows // LANES)], axis=0
    )
    angles = pos_col * freq_ref[...]
    cosines = jnp.cos(angles)
    lane_ids = lax.broadcasted_iota(jnp.int32, (rows, HD), 1)
    sines = jnp.where(lane_ids < HALF, -1.0, 1.0) * jnp.sin(angles)

    loads[6].wait()
    loads[7].wait()
    counts = counts_ref[...].astype(F32)
    n_dom, n_mem = counts.shape
    domain_rows = BLOCK * jnp.sum(counts, axis=1, keepdims=True)
    live_total = jnp.sum(domain_rows, axis=0, keepdims=True)
    ratio = to_column(ratios_ref[...].astype(F32), n_dom)
    factor = ratio / jnp.sum(ratio, axis=0, keepdims=True) * live_total / domain_rows
    dom_ids = lax.broadcasted_iota(jnp.int32, (n_dom, 1), 0)
    own_factor = jnp.sum(jnp.where(dom_ids == dom, factor, 0.0), axis=0, keepdims=True)
    at_dom = lax.broadcasted_iota(jnp.int32, (n_dom, n_mem), 0) == dom
    at_mem = lax.broadcasted_iota(jnp.int32, (n_dom, n_mem), 1) == fsdp
    own_count = jnp.sum(
        jnp.sum(jnp.where(at_dom & at_mem, counts, 0.0), axis=1, keepdims=True),
        axis=0,
        keepdims=True,
    )
    row_ids = lax.broadcasted_iota(jnp.int32, (rows, 1), 0).astype(F32)
    row_factor = jnp.where(row_ids < BLOCK * own_count, own_factor, 0.0)

    loads[0].wait()
    token = tokens_ref[...].astype(F32)
    mean_square = jnp.sum(token * token, axis=1, keepdims=True) * (1.0 / width)
    inv_norm = lax.rsqrt(mean_square + 1e-06)

    loads[1].wait()
    scale = row_factor * inv_norm
    for h in range(2 * heads):
        part = cot_ref[:, h * HD : (h + 1) * HD].astype(F32) * scale
        if h < heads:
            part = part * cosines - pltpu.roll(part, HALF, 1) * sines
        upstream[:, h * HD : (h + 1) * HD] = part.astype(BF16)

    pl.semaphore_wait(barrier, 2 * plane - 1 + 2 + ring - near_self)

    def g1_copy(t):
        return remote(
            own_gw.at[:, lane_tile(y)],
            land_g1.at[x_lo],
            sem_g1s.at[t],
            sem_g1r.at[x_lo],
            dev(x_hi * 2 + t, y, core, wrap_z(z + q - 4 * t)),
        )

    g1_local = pltpu.make_async_copy(
        own_gw.at[:, lane_tile(y)], land_g1.at[0], sem_g1r.at[0]
    )

    @pl.when(own_class != 0)
    def _():
        g1_copy(0).start()

    @pl.when(own_class == 0)
    def _():
        g1_local.start()

    g1_copy(1).start()

    sibling = dev(x, y, 1 - core, z)

    def r0_copy(j):
        return remote(
            part_m.at[j, :, lo_sib],
            land_r0.at[j],
            sem_r0s.at[j],
            sem_r0r.at[j],
            sibling,
        )

    def m_step(j, carry):
        lhs = tokens_ref[:, pl.ds(pl.multiple_of(j * group, group), group)]
        prod = lax.dot_general(
            lhs, upstream[...], (((0,), (0,)), ((), ())), preferred_element_type=F32
        )
        part_m[j] = prod.reshape(4, 2, slab, cols).astype(BF16)
        r0_copy(j).start()
        return carry

    lax.fori_loop(0, jn, m_step, 0)

    def neighbour(k):
        return lax.rem(x + k // ny, 4), lax.rem(y + lax.rem(k, ny), ny)

    def r1_copy(k, j):
        xx, yy = neighbour(k)
        to_class = (xx // 2) * 2 + core + 4 * lax.rem(xx, 2)
        hi = lax.rem(z - to_class + 2 * nz, 8) // 2
        return remote(
            sum_r0.at[j, hi, :, lane_tile(yy)],
            land_r1.at[k, j],
            sem_r1s.at[k, j],
            sem_r1r.at[k, j],
            dev(xx, yy, core, z),
        )

    def r1_send(j, carry):
        r0_copy(j).wait_recv()
        total = part_m[j, :, lo_own].astype(F32) + land_r0[j].astype(F32)
        sum_r0[j] = total.astype(BF16)

        def one(k, c):
            r1_copy(k, j).start()
            return c

        return lax.fori_loop(1, plane, one, carry)

    lax.fori_loop(0, jn, r1_send, 0)

    for half in range(2):
        pltpu.make_async_copy(
            land_g1.at[half], land_g1.at[half], sem_g1r.at[half]
        ).wait()
    piece_g[home] = jnp.concatenate(
        [land_g1[0].astype(F32), land_g1[1].astype(F32)], axis=0
    ).astype(BF16)

    def ring_copy(i, at, device):
        return remote(
            piece_g.at[at], piece_g.at[at], sem_gxs.at[i], sem_gxr.at[i], device
        )

    def nth(i):
        return lax.rem(home + i + 2 * jn, jn)

    if jn > 1:
        ring_copy(0, home, ahead).start()
    if jn > 2:
        ring_copy(1, home, behind).start()

    def r1_arrive(j, carry):
        def one(k, total):
            r1_copy(k, j).wait_recv()
            return total + land_r1[k, j].astype(F32)

        total = lax.fori_loop(
            1, plane, one, sum_r0[j, hi_own, :, lane_tile(y)].astype(F32)
        )
        for half in range(2):
            sum_r1[j, half] = total[half * shard : (half + 1) * shard, :].astype(BF16)
        return carry

    lax.fori_loop(0, jn // 2, r1_arrive, 0)
    if jn > 1:
        ring_copy(0, nth(-1), behind).wait_recv()
    if jn > 3:
        ring_copy(2, nth(-1), ahead).start()
    lax.fori_loop(jn // 2, jn, r1_arrive, 0)
    if jn > 2:
        ring_copy(1, nth(1), ahead).wait_recv()
    if jn > 3:
        ring_copy(2, nth(2), behind).wait_recv()

    def r2_copy(i):
        a, half = i // 2, lax.rem(i, 2)
        far = 8 * a + residue
        slot = 2 * (wrap_z(z - own_class - far) // 8) + x_lo
        return (
            (far == z) & (half == x_lo),
            remote(
                sum_r1.at[a, half],
                land_r2.at[slot],
                sem_r2s.at[i],
                sem_r2r.at[slot],
                dev(x_hi * 2 + half, y, core, far),
            ),
        )

    r2_local = pltpu.make_async_copy(
        sum_r1.at[z // 8, x_lo], land_r2.at[0], sem_r2r.at[0]
    )

    def r2_start(i, carry):
        stays, copy = r2_copy(i)

        @pl.when(jnp.logical_not(stays))
        def _():
            copy.start()

        @pl.when(stays)
        def _():
            r2_local.start()

        return carry

    lax.fori_loop(0, steps, r2_start, 0)

    def g2_copy(k):
        xx, yy = neighbour(k)
        return remote(
            piece_g,
            full_gw.at[:, hi_own, lo_own, :, lane_tile(y)],
            sem_g2s.at[k],
            sem_g2r.at[k],
            dev(xx, yy, core, z),
        )

    g2_local = pltpu.make_async_copy(
        piece_g, full_gw.at[:, hi_own, lo_own, :, lane_tile(y)], sem_g2r.at[0]
    )
    g2_local.start()

    def g2_start(k, carry):
        g2_copy(k).start()
        return carry

    lax.fori_loop(1, plane, g2_start, 0)

    def g3_copy(k, lo):
        xx = lax.rem(x - k // ny + 4, 4)
        yy = lax.rem(y - lax.rem(k, ny) + ny, ny)
        from_class = (xx // 2) * 2 + 4 * lax.rem(xx, 2) + lax.rem(core + lo_own + lo, 2)
        hi = lax.rem(z - from_class + 2 * nz, 8) // 2
        view = full_gw.at[:, hi, lo, :, lane_tile(yy)]
        return remote(view, view, sem_g3s.at[k], sem_g3r.at[k], sibling)

    g2_local.wait()
    g3_copy(0, lo_own).start()

    def g2_arrive(k, carry):
        g2_copy(k).wait_recv()
        g3_copy(k, lo_own).start()
        return carry

    lax.fori_loop(1, plane, g2_arrive, 0)

    def r2_arrive(s, total):
        pltpu.make_async_copy(land_r2.at[s], land_r2.at[s], sem_r2r.at[s]).wait()
        return total + land_r2[s].astype(F32)

    sum_r2[...] = lax.fori_loop(0, steps, r2_arrive, jnp.zeros((shard, LANES), F32))

    def r3_copy(i):
        hh = lax.rem(x_hi + i // (2 * ny), 2)
        yy = lax.rem(y + lax.rem(i // 2, ny), ny)
        cc = lax.rem(core + lax.rem(i, 2), 2)
        return remote(
            sum_r2,
            land_r3.at[q, :, lane_tile(y)],
            sem_r3s.at[i],
            sem_r3r.at[i],
            dev(hh * 2 + x_lo, yy, cc, z),
        )

    r3_local = pltpu.make_async_copy(
        sum_r2, land_r3.at[q, :, lane_tile(y)], sem_r3r.at[0]
    )
    r3_local.start()

    def r3_start(i, carry):
        r3_copy(i).start()
        return carry

    lax.fori_loop(1, plane, r3_start, 0)

    def g3_arrive(k, carry):
        g3_copy(k, lo_sib).wait_recv()
        return carry

    lax.fori_loop(0, plane, g3_arrive, 0)

    def p_step(j, total):
        lhs = tokens_ref[:, pl.ds(pl.multiple_of(j * group, group), group)]
        rhs = full_gw[j].reshape(group, cols)
        return total + jnp.dot(lhs, rhs, preferred_element_type=F32)

    projected = lax.fori_loop(0, jn, p_step, jnp.zeros((rows, cols), F32))
    projected = projected * inv_norm
    for h in range(2 * heads):
        part = projected[:, h * HD : (h + 1) * HD]
        if h < heads:
            part = part * cosines + pltpu.roll(part, HALF, 1) * sines
        kv_ref[:, h * HD : (h + 1) * HD] = part.astype(BF16)

    r3_local.wait()

    def r3_arrive(i, carry):
        r3_copy(i).wait_recv()
        return carry

    lax.fori_loop(1, plane, r3_arrive, 0)
    total = land_r3[0] + land_r3[1] + land_r3[2] + land_r3[3]
    root = jnp.sqrt(live_total)
    wg_ref[...] = total * gain_col / root
    gain_sum = jnp.sum(total * weight, axis=1, keepdims=True)
    gg_ref[...] = to_row(gain_sum / root, shard)

    @pl.when(own_class != 0)
    def _():
        g1_copy(0).wait_send()

    g1_copy(1).wait_send()
    for i in range(min(jn - 1, 3)):
        ring_copy(i, home, ahead).wait_send()

    def r2_drain(i, carry):
        stays, copy = r2_copy(i)

        @pl.when(jnp.logical_not(stays))
        def _():
            copy.wait_send()

        return carry

    def r0_drain(j, carry):
        r0_copy(j).wait_send()
        return carry

    def drain(k, carry):
        g2_copy(k).wait_send()
        r3_copy(k).wait_send()

        def one(j, c):
            r1_copy(k, j).wait_send()
            return c

        return lax.fori_loop(0, jn, one, carry)

    def g3_drain(k, carry):
        g3_copy(k, lo_own).wait_send()
        return carry

    lax.fori_loop(0, steps, r2_drain, 0)
    lax.fori_loop(0, jn, r0_drain, 0)
    lax.fori_loop(1, plane, drain, 0)
    lax.fori_loop(0, plane, g3_drain, 0)


def body(ny, nz, tokens, gain, kv_weight, positions, cotangent, counts, ratios):
    rows, width = tokens.shape
    shard, cols = kv_weight.shape
    jn, plane = nz // 8, 4 * ny
    steps = 2 * jn
    slab = 2 * shard
    exponents = np.arange(HALF) * (2.0 / HD)
    freq = np.power(1000000.0, -exponents).astype(np.float32)
    freq = jnp.asarray(np.concatenate([freq, freq])[None, :])
    operands = (
        counts,
        ratios.reshape(1, -1),
        gain.reshape(1, -1),
        kv_weight,
        positions.reshape(-1, LANES),
        freq,
        tokens,
        cotangent,
    )
    vmem = pl.BlockSpec(memory_space=pltpu.VMEM)
    dma = pltpu.SemaphoreType.DMA
    kv, wg, gg = pl.pallas_call(
        functools.partial(kernel, ny, nz),
        out_shape=(
            jax.ShapeDtypeStruct((rows, cols), BF16),
            jax.ShapeDtypeStruct((shard, cols), F32),
            jax.ShapeDtypeStruct((1, shard), F32),
        ),
        in_specs=[pl.BlockSpec(memory_space=pltpu.HBM)] * len(operands),
        out_specs=(vmem, vmem, vmem),
        scratch_shapes=[pltpu.VMEM(v.shape, v.dtype) for v in operands]
        + [
            pltpu.VMEM((shard, cols), BF16),
            pltpu.VMEM((2, shard, LANES), BF16),
            pltpu.VMEM((jn, slab, LANES), BF16),
            pltpu.VMEM((jn, 4, 2, slab, cols), BF16),
            pltpu.VMEM((jn, 4, 2, slab, cols), BF16),
            pltpu.VMEM((jn, 4, slab, cols), BF16),
            pltpu.VMEM((jn, 4, slab, cols), BF16),
            pltpu.VMEM((plane, jn, slab, LANES), BF16),
            pltpu.VMEM((jn, 2, shard, LANES), BF16),
            pltpu.VMEM((steps, shard, LANES), BF16),
            pltpu.VMEM((shard, LANES), F32),
            pltpu.VMEM((4, shard, cols), F32),
            pltpu.VMEM((rows, cols), BF16),
            dma((len(operands),)),
            dma((2,)),
            dma((2,)),
            dma((3,)),
            dma((3,)),
            dma((plane,)),
            dma((plane,)),
            dma((plane,)),
            dma((plane,)),
            dma((jn,)),
            dma((jn,)),
            dma((plane, jn)),
            dma((plane, jn)),
            dma((steps,)),
            dma((steps,)),
            dma((plane,)),
            dma((plane,)),
        ],
        compiler_params=pltpu.CompilerParams(
            collective_id=0, has_side_effects=True, vmem_limit_bytes=56 * 2**20
        ),
        name="kv_exchange",
    )(*operands)
    return (kv, wg, gg.reshape(-1))


def solution(mesh):
    ny = mesh.shape["dom"] // 4
    nz = mesh.shape["fsdp"] // 2
    return jax.shard_map(
        functools.partial(body, ny, nz),
        mesh=mesh,
        in_specs=(
            P(("dom", "fsdp"), None),
            P("fsdp"),
            P("fsdp", None),
            P(("dom", "fsdp")),
            P(("dom", "fsdp"), None),
            P(),
            P(),
        ),
        out_specs=(P(("dom", "fsdp"), None), P("fsdp", None), P("fsdp")),
        check_vma=False,
    )
```

time: 85.4 us -> 69.3 us (0.81)
  Pallas kernels: 78.3 us -> 65.7 us
  local copies, waits for them, and re-layouts: 6.03 us -> 2.82 us
    pallas_call x1, Pallas kernels: 78.3 us -> 65.7 us  [body(): pl.pallas_call(functools.partial(kernel, ny, nz), out_shape=(jax.ShapeDty...]
    unnamed x19 -> x7, local copies, waits for them, and re-layouts: 6.03 us -> 2.82 us
where the time goes in v2:
time: 69.3 us; the launch traced here: 69.2 us
  Pallas kernels  65.7 us (95%)
  local copies, waits for them, and re-layouts  2.82 us (4%)
    pallas_call x1, Pallas kernels, body(): pl.pallas_call(functools.partial(kernel, ny, nz), out_shape=(jax.ShapeDty...  65.7 us
    unnamed x7, local copies, waits for them, and re-layouts  2.82 us

profile of v2, /device:TPU:1, one launch (start us, length us, event | category | flops | bytes accessed | tf_op | source)
XLA Modules:
  0.0 69.2 jit_solution(15313261560559367971)
XLA Ops:
  0.6 65.7 %kv_exchange.1 = (bf16[256,512]{1,0:T(8,128)(2,1)}, f32[24,512]{1,0:T(8,128)}, f32[1,24]{1,0:T(1,128)}) custom-call(s32[16,64]{1,0:T(8,128)} %counts_hbm.1, s32[1,16]{1,0:T(1,128)} %bitcast.5, bf16[1,24]{1,0:T(2,128)(2,1)} %bitcast.6, bf16[24,512]{1,0:T(8,128)(2,1)} %weight_hbm.1, s32[2,128]{1,0:T(2,128)} %bitcast.4, f32[1,128]{1,0:T(1,128)} %constant.2.clone.freq_hbm, ...), custom_call_target="tpu_custom_call" | custom-call | tf_op jit(solution)/shard_map/kv_exchange/pallas_call | solution.py:548
  66.3 0.0 copy-start
  66.3 1.7 %copy.14 = bf16[256,512]{1,0:T(8,128)(2,1)} copy(bf16[256,512]{1,0:T(8,128)(2,1)} %get-tuple-element.12) | data formatting | bytes 524288
  68.0 0.0 copy-done
  68.0 0.0 copy-start.1
  68.0 0.6 copy.15
  68.7 0.0 copy-done.1
  68.7 0.5 copy.16
Async XLA Ops:
  66.3 1.7 %copy-start = (f32[24,512]{1,0:T(8,128)S(1)}, f32[24,512]{1,0:T(8,128)}, u32[]{:S(2)}) copy-start(f32[24,512]{1,0:T(8,128)} %get-tuple-element.13) | copy-start | bytes 147460
  68.0 0.6 copy-start.1

commit v3 on v2

--- a/solution.py
+++ b/solution.py
@@ -42,9 +42,9 @@
     freq_hbm,
     tokens_hbm,
     cot_hbm,
-    kv_ref,
-    wg_ref,
-    gg_ref,
+    kv_hbm,
+    wg_hbm,
+    gg_hbm,
     counts_ref,
     ratios_ref,
     gain_ref,
@@ -66,7 +66,11 @@
     sum_r2,
     land_r3,
     upstream,
+    kv_ref,
+    wg_ref,
+    gg_ref,
     sem_in,
+    sem_out,
     sem_g1s,
     sem_g1r,
     sem_gxs,
@@ -87,9 +91,9 @@
     dom = lax.axis_index("dom")
     fsdp = lax.axis_index("fsdp")
     core = lax.rem(dom, 2)
-    y = lax.rem(dom // 2, ny)
-    x_hi = dom // (2 * ny)
-    z = fsdp // 2
+    y = lax.rem(lax.div(dom, 2), ny)
+    x_hi = lax.div(dom, 2 * ny)
+    z = lax.div(fsdp, 2)
     x_lo = lax.rem(fsdp, 2)
     x = x_hi * 2 + x_lo
     q = x_hi * 2 + core
@@ -106,7 +110,7 @@
     lo_sib = 1 - lo_own
 
     def dev(xx, yy, cc, zz):
-        return ((xx // 2 * ny + yy) * 2 + cc, zz * 2 + lax.rem(xx, 2))
+        return (lax.div(xx, 2) * (2 * ny) + yy * 2 + cc, zz * 2 + lax.rem(xx, 2))
 
     def remote(src, dst, send, recv, device):
         return pltpu.make_async_remote_copy(
@@ -145,22 +149,33 @@
     own_class = q + 4 * x_lo
     own_shift = q - 4 * x_lo
     residue = lax.rem(z - own_class + 2 * nz, 8)
-    hi_own = residue // 2
-    home = wrap_z(z - own_shift) // 8
+    hi_own = lax.div(residue, 2)
+    home = lax.div(wrap_z(z - own_shift), 8)
 
     barrier = pltpu.get_barrier_semaphore()
 
     def greet(device):
         pl.semaphore_signal(barrier, inc=1, device_id=device, device_id_type=MESH)
 
-    def greet_plane(i, carry):
-        xx = lax.rem(x + i // (2 * ny), 4)
-        yy = lax.rem(y + lax.rem(i // 2, ny), ny)
-        cc = lax.rem(core + lax.rem(i, 2), 2)
-        greet(dev(xx, yy, cc, z))
-        return carry
-
-    lax.fori_loop(1, 2 * plane, greet_plane, 0)
+    xs = [lax.rem(x + i, 4) for i in range(4)]
+    ys = [lax.rem(y + i, ny) for i in range(ny)]
+
+    def class_of(xx, cc):
+        return lax.div(xx, 2) * 2 + cc + 4 * lax.rem(xx, 2)
+
+    def hi_of(xx, cc):
+        return lax.div(lax.rem(z - class_of(xx, cc) + 2 * nz, 8), 2)
+
+    his = [hi_of(xx, core) for xx in xs]
+    at_plane = [[dev(xx, yy, core, z) for yy in ys] for xx in xs]
+    at_other = [[(a + 1 - 2 * core, b) for a, b in line] for line in at_plane]
+    sibling = at_other[0][0]
+    peers = [(i, j) for i in range(4) for j in range(ny)][1:]
+
+    greet(sibling)
+    for i, j in peers:
+        greet(at_plane[i][j])
+        greet(at_other[i][j])
     near_self = (own_class == 0).astype(jnp.int32)
     for half in range(2):
         owner = dev(x_hi * 2 + half, y, core, wrap_z(z - own_shift))
@@ -255,15 +270,9 @@
 
     g1_copy(1).start()
 
-    sibling = dev(x, y, 1 - core, z)
-
     def r0_copy(j):
         return remote(
-            part_m.at[j, :, lo_sib],
-            land_r0.at[j],
-            sem_r0s.at[j],
-            sem_r0r.at[j],
-            sibling,
+            part_m.at[j, :, lo_sib], land_r0.at[j], sem_r0s, sem_r0r.at[j], sibling
         )
 
     def m_step(j, carry):
@@ -277,31 +286,19 @@
 
     lax.fori_loop(0, jn, m_step, 0)
 
-    def neighbour(k):
-        return lax.rem(x + k // ny, 4), lax.rem(y + lax.rem(k, ny), ny)
-
-    def r1_copy(k, j):
-        xx, yy = neighbour(k)
-        to_class = (xx // 2) * 2 + core + 4 * lax.rem(xx, 2)
-        hi = lax.rem(z - to_class + 2 * nz, 8) // 2
-        return remote(
-            sum_r0.at[j, hi, :, lane_tile(yy)],
-            land_r1.at[k, j],
-            sem_r1s.at[k, j],
-            sem_r1r.at[k, j],
-            dev(xx, yy, core, z),
-        )
-
     def r1_send(j, carry):
         r0_copy(j).wait_recv()
         total = part_m[j, :, lo_own].astype(F32) + land_r0[j].astype(F32)
         sum_r0[j] = total.astype(BF16)
-
-        def one(k, c):
-            r1_copy(k, j).start()
-            return c
-
-        return lax.fori_loop(1, plane, one, carry)
+        for k, (dx, dy) in enumerate(peers):
+            remote(
+                sum_r0.at[j, his[dx], :, lane_tile(ys[dy])],
+                land_r1.at[j, k],
+                sem_r1s,
+                sem_r1r.at[j],
+                at_plane[dx][dy],
+            ).start()
+        return carry
 
     lax.fori_loop(0, jn, r1_send, 0)
 
@@ -326,136 +323,108 @@
     if jn > 2:
         ring_copy(1, home, behind).start()
 
+    def arrived(buffer, sem):
+        pltpu.make_async_copy(buffer, buffer, sem).wait()
+
     def r1_arrive(j, carry):
-        def one(k, total):
-            r1_copy(k, j).wait_recv()
-            return total + land_r1[k, j].astype(F32)
-
-        total = lax.fori_loop(
-            1, plane, one, sum_r0[j, hi_own, :, lane_tile(y)].astype(F32)
-        )
+        arrived(land_r1.at[j], sem_r1r.at[j])
+
+        total = sum_r0[j, hi_own, :, lane_tile(y)].astype(F32)
+        for k in range(plane - 1):
+            total = total + land_r1[j, k].astype(F32)
         for half in range(2):
             sum_r1[j, half] = total[half * shard : (half + 1) * shard, :].astype(BF16)
         return carry
 
-    lax.fori_loop(0, jn // 2, r1_arrive, 0)
+    lax.fori_loop(0, 1, r1_arrive, 0)
     if jn > 1:
         ring_copy(0, nth(-1), behind).wait_recv()
     if jn > 3:
         ring_copy(2, nth(-1), ahead).start()
-    lax.fori_loop(jn // 2, jn, r1_arrive, 0)
+    lax.fori_loop(1, jn, r1_arrive, 0)
     if jn > 2:
         ring_copy(1, nth(1), ahead).wait_recv()
     if jn > 3:
         ring_copy(2, nth(2), behind).wait_recv()
 
-    def r2_copy(i):
-        a, half = i // 2, lax.rem(i, 2)
-        far = 8 * a + residue
-        slot = 2 * (wrap_z(z - own_class - far) // 8) + x_lo
-        return (
-            (far == z) & (half == x_lo),
-            remote(
-                sum_r1.at[a, half],
-                land_r2.at[slot],
-                sem_r2s.at[i],
-                sem_r2r.at[slot],
-                dev(x_hi * 2 + half, y, core, far),
-            ),
+    order = sorted(range(jn), key=lambda i: -min(i, jn - i))
+
+    def r2_copy(i, half):
+        far = wrap_z(z - own_shift + 8 * i)
+        slot = 2 * lax.div(wrap_z(z - own_class - far), 8) + x_lo
+        return remote(
+            sum_r1.at[nth(i), half],
+            land_r2.at[slot],
+            sem_r2s,
+            sem_r2r,
+            dev(x_hi * 2 + half, y, core, far),
         )
 
     r2_local = pltpu.make_async_copy(
-        sum_r1.at[z // 8, x_lo], land_r2.at[0], sem_r2r.at[0]
-    )
-
-    def r2_start(i, carry):
-        stays, copy = r2_copy(i)
-
-        @pl.when(jnp.logical_not(stays))
-        def _():
-            copy.start()
-
-        @pl.when(stays)
-        def _():
-            r2_local.start()
-
-        return carry
-
-    lax.fori_loop(0, steps, r2_start, 0)
-
-    def g2_copy(k):
-        xx, yy = neighbour(k)
-        return remote(
-            piece_g,
-            full_gw.at[:, hi_own, lo_own, :, lane_tile(y)],
-            sem_g2s.at[k],
-            sem_g2r.at[k],
-            dev(xx, yy, core, z),
-        )
-
-    g2_local = pltpu.make_async_copy(
-        piece_g, full_gw.at[:, hi_own, lo_own, :, lane_tile(y)], sem_g2r.at[0]
-    )
-    g2_local.start()
-
-    def g2_start(k, carry):
-        g2_copy(k).start()
-        return carry
-
-    lax.fori_loop(1, plane, g2_start, 0)
-
-    def g3_copy(k, lo):
-        xx = lax.rem(x - k // ny + 4, 4)
-        yy = lax.rem(y - lax.rem(k, ny) + ny, ny)
-        from_class = (xx // 2) * 2 + 4 * lax.rem(xx, 2) + lax.rem(core + lo_own + lo, 2)
-        hi = lax.rem(z - from_class + 2 * nz, 8) // 2
-        view = full_gw.at[:, hi, lo, :, lane_tile(yy)]
-        return remote(view, view, sem_g3s.at[k], sem_g3r.at[k], sibling)
-
-    g2_local.wait()
-    g3_copy(0, lo_own).start()
-
-    def g2_arrive(k, carry):
-        g2_copy(k).wait_recv()
-        g3_copy(k, lo_own).start()
-        return carry
-
-    lax.fori_loop(1, plane, g2_arrive, 0)
-
-    def r2_arrive(s, total):
-        pltpu.make_async_copy(land_r2.at[s], land_r2.at[s], sem_r2r.at[s]).wait()
-        return total + land_r2[s].astype(F32)
-
-    sum_r2[...] = lax.fori_loop(0, steps, r2_arrive, jnp.zeros((shard, LANES), F32))
-
-    def r3_copy(i):
-        hh = lax.rem(x_hi + i // (2 * ny), 2)
-        yy = lax.rem(y + lax.rem(i // 2, ny), ny)
-        cc = lax.rem(core + lax.rem(i, 2), 2)
-        return remote(
-            sum_r2,
-            land_r3.at[q, :, lane_tile(y)],
-            sem_r3s.at[i],
-            sem_r3r.at[i],
-            dev(hh * 2 + x_lo, yy, cc, z),
-        )
-
-    r3_local = pltpu.make_async_copy(
-        sum_r2, land_r3.at[q, :, lane_tile(y)], sem_r3r.at[0]
-    )
-    r3_local.start()
-
-    def r3_start(i, carry):
-        r3_copy(i).start()
-        return carry
-
-    lax.fori_loop(1, plane, r3_start, 0)
-
-    def g3_arrive(k, carry):
-        g3_copy(k, lo_sib).wait_recv()
-        return carry
-
-    lax.fori_loop(0, plane, g3_arrive, 0)
+        sum_r1.at[home, 0], land_r2.at[0], sem_r2r
+    )
+    for i in order:
+        for half in range(2):
+            if i == 0 and half == 0:
+
+                @pl.when(own_class != 0)
+                def _():
+                    r2_copy(0, 0).start()
+
+                @pl.when(own_class == 0)
+                def _():
+                    r2_local.start()
+
+            else:
+                r2_copy(i, half).start()
+
+    g2_view = full_gw.at[:, hi_own, lo_own, :, lane_tile(y)]
+    pltpu.make_async_copy(piece_g, g2_view, sem_g2r.at[0]).start()
+    for dx, dy in peers:
+        remote(piece_g, g2_view, sem_g2s, sem_g2r.at[dx], at_plane[dx][dy]).start()
+
+    arrived(land_r0, sem_r0s)
+    arrived(land_r1, sem_r1s)
+
+    @pl.when(own_class != 0)
+    def _():
+        g1_copy(0).wait_send()
+
+    g1_copy(1).wait_send()
+    for i in range(min(jn - 1, 3)):
+        ring_copy(i, home, ahead).wait_send()
+
+    def g3_copy(hi, lo, i):
+        view = full_gw.at[:, hi, lo]
+        return remote(view, view, sem_g3s, sem_g3r.at[i], sibling)
+
+    for dx in range(4):
+        back = (4 - dx) % 4
+        arrived(full_gw.at[:, his[back], lo_own], sem_g2r.at[dx])
+        g3_copy(his[back], lo_own, dx).start()
+
+    arrived(land_r2, sem_r2r)
+    total2 = land_r2[0].astype(F32)
+    for s in range(1, steps):
+        total2 = total2 + land_r2[s].astype(F32)
+    sum_r2[...] = total2
+
+    slot3 = 4 * y + q
+    pltpu.make_async_copy(sum_r2, land_r3.at[slot3], sem_r3r).start()
+
+    def r3_send(device):
+        remote(sum_r2, land_r3.at[slot3], sem_r3s, sem_r3r, device).start()
+
+    r3_send(sibling)
+    for dx in (0, 2):
+        for dy in range(ny):
+            if dx or dy:
+                r3_send(at_plane[dx][dy])
+                r3_send(at_other[dx][dy])
+
+    for dx in range(4):
+        back = (4 - dx) % 4
+        arrived(full_gw.at[:, hi_of(xs[back], 1 - core), lo_sib], sem_g3r.at[dx])
 
     def p_step(j, total):
         lhs = tokens_ref[:, pl.ds(pl.multiple_of(j * group, group), group)]
@@ -469,59 +438,56 @@
         if h < heads:
             part = part * cosines + pltpu.roll(part, HALF, 1) * sines
         kv_ref[:, h * HD : (h + 1) * HD] = part.astype(BF16)
-
-    r3_local.wait()
-
-    def r3_arrive(i, carry):
-        r3_copy(i).wait_recv()
-        return carry
-
-    lax.fori_loop(1, plane, r3_arrive, 0)
-    total = land_r3[0] + land_r3[1] + land_r3[2] + land_r3[3]
+    kv_out = pltpu.make_async_copy(kv_ref, kv_hbm, sem_out.at[0])
+    kv_out.start()
+
+    arrived(land_r3, sem_r3r)
     root = jnp.sqrt(live_total)
-    wg_ref[...] = total * gain_col / root
-    gain_sum = jnp.sum(total * weight, axis=1, keepdims=True)
+    gain_sum = jnp.zeros((shard, 1), F32)
+    for i in range(ny):
+        tile = slice(i * LANES, (i + 1) * LANES)
+        total3 = land_r3[4 * i] + land_r3[4 * i + 1] + land_r3[4 * i + 2] + land_r3[4 * i + 3]
+        wg_ref[:, tile] = total3 * gain_col / root
+        gain_sum = gain_sum + jnp.sum(total3 * weight[:, tile], axis=1, keepdims=True)
+    wg_out = pltpu.make_async_copy(wg_ref, wg_hbm, sem_out.at[1])
+    wg_out.start()
     gg_ref[...] = to_row(gain_sum / root, shard)
+    gg_out = pltpu.make_async_copy(gg_ref, gg_hbm, sem_out.at[2])
+    gg_out.start()
+
+    arrived(land_r1, sem_g2s)
+    arrived(full_gw.at[:, :, lo_own], sem_g3s)
 
     @pl.when(own_class != 0)
     def _():
-        g1_copy(0).wait_send()
-
-    g1_copy(1).wait_send()
-    for i in range(min(jn - 1, 3)):
-        ring_copy(i, home, ahead).wait_send()
-
-    def r2_drain(i, carry):
-        stays, copy = r2_copy(i)
-
-        @pl.when(jnp.logical_not(stays))
-        def _():
-            copy.wait_send()
-
-        return carry
-
-    def r0_drain(j, carry):
-        r0_copy(j).wait_send()
-        return carry
-
-    def drain(k, carry):
-        g2_copy(k).wait_send()
-        r3_copy(k).wait_send()
-
-        def one(j, c):
-            r1_copy(k, j).wait_send()
-            return c
-
-        return lax.fori_loop(0, jn, one, carry)
-
-    def g3_drain(k, carry):
-        g3_copy(k, lo_own).wait_send()
-        return carry
-
-    lax.fori_loop(0, steps, r2_drain, 0)
-    lax.fori_loop(0, jn, r0_drain, 0)
-    lax.fori_loop(1, plane, drain, 0)
-    lax.fori_loop(0, plane, g3_drain, 0)
+        arrived(land_r2, sem_r2s)
+
+    @pl.when(own_class == 0)
+    def _():
+        arrived(land_r2.at[pl.ds(0, steps - 1)], sem_r2s)
+
+    arrived(land_r3.at[pl.ds(0, plane - 1)], sem_r3s)
+    kv_out.wait()
+    wg_out.wait()
+    gg_out.wait()
+
+
+def copy_kernel(count, *refs):
+    ins, outs, held = refs[:count], refs[count : 2 * count], refs[2 * count : 3 * count]
+    sems = refs[-1]
+    loads = [
+        pltpu.make_async_copy(ins[i], held[i], sems.at[0, i]) for i in range(count)
+    ]
+    stores = [
+        pltpu.make_async_copy(held[i], outs[i], sems.at[1, i]) for i in range(count)
+    ]
+    for load in loads:
+        load.start()
+    for load, store in zip(loads, stores):
+        load.wait()
+        store.start()
+    for store in stores:
+        store.wait()
 
 
 def body(ny, nz, tokens, gain, kv_weight, positions, cotangent, counts, ratios):
@@ -543,17 +509,18 @@
         tokens,
         cotangent,
     )
-    vmem = pl.BlockSpec(memory_space=pltpu.VMEM)
+    hbm = pl.BlockSpec(memory_space=pltpu.HBM)
     dma = pltpu.SemaphoreType.DMA
-    kv, wg, gg = pl.pallas_call(
+    shapes = (
+        jax.ShapeDtypeStruct((rows, cols), BF16),
+        jax.ShapeDtypeStruct((shard, cols), F32),
+        jax.ShapeDtypeStruct((1, shard), F32),
+    )
+    outs = pl.pallas_call(
         functools.partial(kernel, ny, nz),
-        out_shape=(
-            jax.ShapeDtypeStruct((rows, cols), BF16),
-            jax.ShapeDtypeStruct((shard, cols), F32),
-            jax.ShapeDtypeStruct((1, shard), F32),
-        ),
-        in_specs=[pl.BlockSpec(memory_space=pltpu.HBM)] * len(operands),
-        out_specs=(vmem, vmem, vmem),
+        out_shape=shapes,
+        in_specs=[hbm] * len(operands),
+        out_specs=(hbm, hbm, hbm),
         scratch_shapes=[pltpu.VMEM(v.shape, v.dtype) for v in operands]
         + [
             pltpu.VMEM((shard, cols), BF16),
@@ -563,35 +530,48 @@
             pltpu.VMEM((jn, 4, 2, slab, cols), BF16),
             pltpu.VMEM((jn, 4, slab, cols), BF16),
             pltpu.VMEM((jn, 4, slab, cols), BF16),
-            pltpu.VMEM((plane, jn, slab, LANES), BF16),
+            pltpu.VMEM((jn, plane - 1, slab, LANES), BF16),
             pltpu.VMEM((jn, 2, shard, LANES), BF16),
             pltpu.VMEM((steps, shard, LANES), BF16),
             pltpu.VMEM((shard, LANES), F32),
-            pltpu.VMEM((4, shard, cols), F32),
+            pltpu.VMEM((plane, shard, LANES), F32),
             pltpu.VMEM((rows, cols), BF16),
+        ]
+        + [pltpu.VMEM(v.shape, v.dtype) for v in shapes]
+        + [
             dma((len(operands),)),
+            dma((3,)),
             dma((2,)),
             dma((2,)),
             dma((3,)),
             dma((3,)),
-            dma((plane,)),
-            dma((plane,)),
-            dma((plane,)),
-            dma((plane,)),
+            dma,
+            dma((4,)),
+            dma,
+            dma((4,)),
+            dma,
             dma((jn,)),
+            dma,
             dma((jn,)),
-            dma((plane, jn)),
-            dma((plane, jn)),
-            dma((steps,)),
-            dma((steps,)),
-            dma((plane,)),
-            dma((plane,)),
+            dma,
+            dma,
+            dma,
+            dma,
         ],
         compiler_params=pltpu.CompilerParams(
             collective_id=0, has_side_effects=True, vmem_limit_bytes=56 * 2**20
         ),
         name="kv_exchange",
     )(*operands)
+    kv, wg, gg = pl.pallas_call(
+        functools.partial(copy_kernel, len(outs)),
+        out_shape=shapes,
+        in_specs=[hbm] * len(outs),
+        out_specs=(hbm, hbm, hbm),
+        scratch_shapes=[pltpu.VMEM(v.shape, v.dtype) for v in shapes]
+        + [dma((2, len(outs)))],
+        name="kv_outputs",
+    )(*outs)
     return (kv, wg, gg.reshape(-1))
 
 

time: 69.3 us -> 63.9 us (0.922)
  local copies, waits for them, and re-layouts: 2.82 us -> 0 us
  Pallas kernels: 65.7 us -> 63.1 us
    unnamed x7 -> x0, local copies, waits for them, and re-layouts: 2.82 us -> none
    pallas_call x1 -> x2, Pallas kernels: 65.7 us -> 63.1 us  [the longest x1 61.4 us: body(): pl.pallas_call(functools.partial(kernel, ny, nz), out_shape=shapes, in_sp...]
where the time goes in v3:
time: 63.9 us; the launch traced here: 63.7 us
  Pallas kernels  63.1 us (99%)
  between operations  0.64 us (1%)
    pallas_call x1, Pallas kernels, body(): pl.pallas_call(functools.partial(kernel, ny, nz), out_shape=shapes, in_sp...  61.4 us
    pallas_call x1, Pallas kernels, body(): pl.pallas_call(functools.partial(copy_kernel, len(outs)), out_shape=shape...  1.71 us

profile of v3, /device:TPU:1, one launch (start us, length us, event | category | flops | bytes accessed | tf_op | source)
XLA Modules:
  0.0 63.7 jit_solution(550024533782043888)
XLA Ops:
  0.6 61.4 %kv_exchange.1 = (bf16[256,512]{1,0:T(8,128)(2,1)}, f32[24,512]{1,0:T(8,128)}, f32[1,24]{1,0:T(1,128)}) custom-call(s32[16,64]{1,0:T(8,128)} %counts_hbm.1, s32[1,16]{1,0:T(1,128)} %bitcast.5, bf16[1,24]{1,0:T(2,128)(2,1)} %bitcast.6, bf16[24,512]{1,0:T(8,128)(2,1)} %weight_hbm.1, s32[2,128]{1,0:T(2,128)} %bitcast.4, f32[1,128]{1,0:T(1,128)} %constant.2.clone.freq_hbm, ...), custom_call_target="tpu_custom_call" | custom-call | tf_op jit(solution)/shard_map/kv_exchange/pallas_call | solution.py:519
  62.0 1.7 %kv_outputs.1 = (bf16[256,512]{1,0:T(8,128)(2,1)}, f32[24,512]{1,0:T(8,128)}, f32[1,24]{1,0:T(1,128)}) custom-call(bf16[256,512]{1,0:T(8,128)(2,1)} %get-tuple-element.9.refs_0_, f32[24,512]{1,0:T(8,128)} %get-tuple-element.10.refs_1_, f32[1,24]{1,0:T(1,128)} %get-tuple-element.11.refs_2_), custom_call_target="tpu_custom_call" | custom-call | tf_op jit(solution)/shard_map/kv_outputs/pallas_call | solution.py:566

commit v4 on v3

--- a/solution.py
+++ b/solution.py
@@ -42,9 +42,9 @@
     freq_hbm,
     tokens_hbm,
     cot_hbm,
-    kv_hbm,
-    wg_hbm,
-    gg_hbm,
+    kv_ref,
+    wg_ref,
+    gg_ref,
     counts_ref,
     ratios_ref,
     gain_ref,
@@ -66,11 +66,7 @@
     sum_r2,
     land_r3,
     upstream,
-    kv_ref,
-    wg_ref,
-    gg_ref,
     sem_in,
-    sem_out,
     sem_g1s,
     sem_g1r,
     sem_gxs,
@@ -87,6 +83,8 @@
     sem_r2r,
     sem_r3s,
     sem_r3r,
+    sem_in_ring,
+    sem_in_far,
 ):
     dom = lax.axis_index("dom")
     fsdp = lax.axis_index("fsdp")
@@ -171,11 +169,13 @@
     at_other = [[(a + 1 - 2 * core, b) for a, b in line] for line in at_plane]
     sibling = at_other[0][0]
     peers = [(i, j) for i in range(4) for j in range(ny)][1:]
+    peers.sort(key=lambda p: (min(p[0], 4 - p[0]) + min(p[1], ny - p[1]), sum(p)))
 
     greet(sibling)
     for i, j in peers:
         greet(at_plane[i][j])
-        greet(at_other[i][j])
+        if i % 2 == 0:
+            greet(at_other[i][j])
     near_self = (own_class == 0).astype(jnp.int32)
     for half in range(2):
         owner = dev(x_hi * 2 + half, y, core, wrap_z(z - own_shift))
@@ -187,6 +187,16 @@
 
         else:
             greet(owner)
+    for t in range(2):
+        near = dev(x_hi * 2 + t, y, core, wrap_z(z + q - 4 * t))
+        if t == 0:
+
+            @pl.when(own_class != 0)
+            def _(near=near):
+                greet(near)
+
+        else:
+            greet(near)
     ring = min(jn - 1, 2)
     ahead = dev(x, y, core, wrap_z(z + 8))
     behind = dev(x, y, core, wrap_z(z - 8))
@@ -245,7 +255,15 @@
             part = part * cosines - pltpu.roll(part, HALF, 1) * sines
         upstream[:, h * HD : (h + 1) * HD] = part.astype(BF16)
 
-    pl.semaphore_wait(barrier, 2 * plane - 1 + 2 + ring - near_self)
+    pl.semaphore_wait(barrier, plane + plane // 2 - 1 + 4 + ring - 2 * near_self)
+
+    def tell(sem, device):
+        pl.semaphore_signal(sem, inc=1, device_id=device, device_id_type=MESH)
+
+    if jn > 1:
+        tell(sem_in_ring, ahead)
+    if jn > 2:
+        tell(sem_in_ring, behind)
 
     def g1_copy(t):
         return remote(
@@ -283,8 +301,6 @@
         part_m[j] = prod.reshape(4, 2, slab, cols).astype(BF16)
         r0_copy(j).start()
         return carry
-
-    lax.fori_loop(0, jn, m_step, 0)
 
     def r1_send(j, carry):
         r0_copy(j).wait_recv()
@@ -300,7 +316,13 @@
             ).start()
         return carry
 
-    lax.fori_loop(0, jn, r1_send, 0)
+    m_step(0, 0)
+
+    def m_and_r1(j, carry):
+        m_step(j, carry)
+        return r1_send(j - 1, carry)
+
+    lax.fori_loop(1, jn, m_and_r1, 0)
 
     for half in range(2):
         pltpu.make_async_copy(
@@ -323,12 +345,17 @@
     if jn > 2:
         ring_copy(1, home, behind).start()
 
+    r1_send(jn - 1, 0)
+    if jn > 1:
+        pl.semaphore_wait(sem_in_ring, ring)
+    if jn > 3:
+        tell(sem_in_far, ahead)
+
     def arrived(buffer, sem):
         pltpu.make_async_copy(buffer, buffer, sem).wait()
 
     def r1_arrive(j, carry):
         arrived(land_r1.at[j], sem_r1r.at[j])
-
         total = sum_r0[j, hi_own, :, lane_tile(y)].astype(F32)
         for k in range(plane - 1):
             total = total + land_r1[j, k].astype(F32)
@@ -336,47 +363,48 @@
             sum_r1[j, half] = total[half * shard : (half + 1) * shard, :].astype(BF16)
         return carry
 
-    lax.fori_loop(0, 1, r1_arrive, 0)
-    if jn > 1:
-        ring_copy(0, nth(-1), behind).wait_recv()
-    if jn > 3:
-        ring_copy(2, nth(-1), ahead).start()
-    lax.fori_loop(1, jn, r1_arrive, 0)
-    if jn > 2:
-        ring_copy(1, nth(1), ahead).wait_recv()
-    if jn > 3:
-        ring_copy(2, nth(2), behind).wait_recv()
-
-    order = sorted(range(jn), key=lambda i: -min(i, jn - i))
-
-    def r2_copy(i, half):
-        far = wrap_z(z - own_shift + 8 * i)
+    def r2_copy(j, half):
+        far = 8 * j + residue
         slot = 2 * lax.div(wrap_z(z - own_class - far), 8) + x_lo
         return remote(
-            sum_r1.at[nth(i), half],
+            sum_r1.at[j, half],
             land_r2.at[slot],
             sem_r2s,
             sem_r2r,
             dev(x_hi * 2 + half, y, core, far),
         )
 
-    r2_local = pltpu.make_async_copy(
-        sum_r1.at[home, 0], land_r2.at[0], sem_r2r
-    )
-    for i in order:
-        for half in range(2):
-            if i == 0 and half == 0:
-
-                @pl.when(own_class != 0)
-                def _():
-                    r2_copy(0, 0).start()
-
-                @pl.when(own_class == 0)
-                def _():
-                    r2_local.start()
-
-            else:
-                r2_copy(i, half).start()
+    def r2_send(j, carry):
+        stays = (own_class == 0) & (j == home)
+
+        @pl.when(jnp.logical_not(stays))
+        def _():
+            r2_copy(j, 0).start()
+
+        @pl.when(stays)
+        def _():
+            pltpu.make_async_copy(sum_r1.at[j, 0], land_r2.at[0], sem_r2r).start()
+
+        r2_copy(j, 1).start()
+        return carry
+
+    def r1_and_r2(j, carry):
+        r1_arrive(j, carry)
+        return r2_send(j, carry)
+
+    early = min(2, jn)
+    lax.fori_loop(0, early, r1_arrive, 0)
+    if jn > 1:
+        ring_copy(0, nth(-1), behind).wait_recv()
+    if jn > 3:
+        ring_copy(2, nth(-1), ahead).start()
+        pl.semaphore_wait(sem_in_far, 1)
+    lax.fori_loop(0, early, r2_send, 0)
+    lax.fori_loop(early, jn, r1_and_r2, 0)
+    if jn > 2:
+        ring_copy(1, nth(1), ahead).wait_recv()
+    if jn > 3:
+        ring_copy(2, nth(2), behind).wait_recv()
 
     g2_view = full_gw.at[:, hi_own, lo_own, :, lane_tile(y)]
     pltpu.make_async_copy(piece_g, g2_view, sem_g2r.at[0]).start()
@@ -393,15 +421,6 @@
     g1_copy(1).wait_send()
     for i in range(min(jn - 1, 3)):
         ring_copy(i, home, ahead).wait_send()
-
-    def g3_copy(hi, lo, i):
-        view = full_gw.at[:, hi, lo]
-        return remote(view, view, sem_g3s, sem_g3r.at[i], sibling)
-
-    for dx in range(4):
-        back = (4 - dx) % 4
-        arrived(full_gw.at[:, his[back], lo_own], sem_g2r.at[dx])
-        g3_copy(his[back], lo_own, dx).start()
 
     arrived(land_r2, sem_r2r)
     total2 = land_r2[0].astype(F32)
@@ -421,6 +440,15 @@
             if dx or dy:
                 r3_send(at_plane[dx][dy])
                 r3_send(at_other[dx][dy])
+
+    def g3_copy(hi, lo, i):
+        view = full_gw.at[:, hi, lo]
+        return remote(view, view, sem_g3s, sem_g3r.at[i], sibling)
+
+    for dx in range(4):
+        back = (4 - dx) % 4
+        arrived(full_gw.at[:, his[back], lo_own], sem_g2r.at[dx])
+        g3_copy(his[back], lo_own, dx).start()
 
     for dx in range(4):
         back = (4 - dx) % 4
@@ -438,8 +466,6 @@
         if h < heads:
             part = part * cosines + pltpu.roll(part, HALF, 1) * sines
         kv_ref[:, h * HD : (h + 1) * HD] = part.astype(BF16)
-    kv_out = pltpu.make_async_copy(kv_ref, kv_hbm, sem_out.at[0])
-    kv_out.start()
 
     arrived(land_r3, sem_r3r)
     root = jnp.sqrt(live_total)
@@ -449,11 +475,7 @@
         total3 = land_r3[4 * i] + land_r3[4 * i + 1] + land_r3[4 * i + 2] + land_r3[4 * i + 3]
         wg_ref[:, tile] = total3 * gain_col / root
         gain_sum = gain_sum + jnp.sum(total3 * weight[:, tile], axis=1, keepdims=True)
-    wg_out = pltpu.make_async_copy(wg_ref, wg_hbm, sem_out.at[1])
-    wg_out.start()
     gg_ref[...] = to_row(gain_sum / root, shard)
-    gg_out = pltpu.make_async_copy(gg_ref, gg_hbm, sem_out.at[2])
-    gg_out.start()
 
     arrived(land_r1, sem_g2s)
     arrived(full_gw.at[:, :, lo_own], sem_g3s)
@@ -467,27 +489,18 @@
         arrived(land_r2.at[pl.ds(0, steps - 1)], sem_r2s)
 
     arrived(land_r3.at[pl.ds(0, plane - 1)], sem_r3s)
-    kv_out.wait()
-    wg_out.wait()
-    gg_out.wait()
 
 
 def copy_kernel(count, *refs):
-    ins, outs, held = refs[:count], refs[count : 2 * count], refs[2 * count : 3 * count]
     sems = refs[-1]
-    loads = [
-        pltpu.make_async_copy(ins[i], held[i], sems.at[0, i]) for i in range(count)
+    copies = [
+        pltpu.make_async_copy(refs[i], refs[count + i], sems.at[i])
+        for i in range(count)
     ]
-    stores = [
-        pltpu.make_async_copy(held[i], outs[i], sems.at[1, i]) for i in range(count)
-    ]
-    for load in loads:
-        load.start()
-    for load, store in zip(loads, stores):
-        load.wait()
-        store.start()
-    for store in stores:
-        store.wait()
+    for copy in copies:
+        copy.start()
+    for copy in copies:
+        copy.wait()
 
 
 def body(ny, nz, tokens, gain, kv_weight, positions, cotangent, counts, ratios):
@@ -510,6 +523,7 @@
         cotangent,
     )
     hbm = pl.BlockSpec(memory_space=pltpu.HBM)
+    vmem = pl.BlockSpec(memory_space=pltpu.VMEM)
     dma = pltpu.SemaphoreType.DMA
     shapes = (
         jax.ShapeDtypeStruct((rows, cols), BF16),
@@ -520,7 +534,7 @@
         functools.partial(kernel, ny, nz),
         out_shape=shapes,
         in_specs=[hbm] * len(operands),
-        out_specs=(hbm, hbm, hbm),
+        out_specs=(vmem, vmem, vmem),
         scratch_shapes=[pltpu.VMEM(v.shape, v.dtype) for v in operands]
         + [
             pltpu.VMEM((shard, cols), BF16),
@@ -536,11 +550,7 @@
             pltpu.VMEM((shard, LANES), F32),
             pltpu.VMEM((plane, shard, LANES), F32),
             pltpu.VMEM((rows, cols), BF16),
-        ]
-        + [pltpu.VMEM(v.shape, v.dtype) for v in shapes]
-        + [
             dma((len(operands),)),
-            dma((3,)),
             dma((2,)),
             dma((2,)),
             dma((3,)),
@@ -557,21 +567,22 @@
             dma,
             dma,
             dma,
+            pltpu.SemaphoreType.REGULAR,
+            pltpu.SemaphoreType.REGULAR,
         ],
         compiler_params=pltpu.CompilerParams(
-            collective_id=0, has_side_effects=True, vmem_limit_bytes=56 * 2**20
+            collective_id=0, has_side_effects=True, vmem_limit_bytes=40 * 2**20
         ),
         name="kv_exchange",
-    )(*operands)
+    )(*[pltpu.with_memory_space_constraint(v, pltpu.HBM) for v in operands])
     kv, wg, gg = pl.pallas_call(
         functools.partial(copy_kernel, len(outs)),
         out_shape=shapes,
-        in_specs=[hbm] * len(outs),
+        in_specs=[vmem] * len(outs),
         out_specs=(hbm, hbm, hbm),
-        scratch_shapes=[pltpu.VMEM(v.shape, v.dtype) for v in shapes]
-        + [dma((2, len(outs)))],
+        scratch_shapes=[dma((len(outs),))],
         name="kv_outputs",
-    )(*outs)
+    )(*[pltpu.with_memory_space_constraint(v, pltpu.VMEM) for v in outs])
     return (kv, wg, gg.reshape(-1))
 
 

time: 63.9 us -> 61.4 us (0.961)
  Pallas kernels: 63.1 us -> 60.6 us
    pallas_call x1, Pallas kernels: 61.4 us -> 59.9 us  [body(): pl.pallas_call(functools.partial(kernel, ny, nz), out_shape=shapes, in_sp...]
    pallas_call x1, Pallas kernels: 1.71 us -> 0.74 us  [body(): pl.pallas_call(functools.partial(copy_kernel, len(outs)), out_shape=shape...]
where the time goes in v4:
time: 61.4 us; the launch traced here: 61.3 us
  Pallas kernels  60.6 us (99%)
  between operations  0.64 us (1%)
    pallas_call x1, Pallas kernels, body(): pl.pallas_call(functools.partial(kernel, ny, nz), out_shape=shapes, in_sp...  59.9 us

profile of v4, /device:TPU:1, one launch (start us, length us, event | category | flops | bytes accessed | tf_op | source)
XLA Modules:
  0.0 61.3 jit_solution(10097709028088124832)
XLA Ops:
  0.6 59.9 %kv_exchange.1 = (bf16[256,512]{1,0:T(8,128)(2,1)S(1)}, f32[24,512]{1,0:T(8,128)S(1)}, f32[1,24]{1,0:T(1,128)S(1)}) custom-call(s32[16,64]{1,0:T(8,128)} %counts_hbm.1, s32[1,16]{1,0:T(1,128)} %bitcast.5, bf16[1,24]{1,0:T(2,128)(2,1)} %bitcast.6, bf16[24,512]{1,0:T(8,128)(2,1)} %weight_hbm.1, s32[2,128]{1,0:T(2,128)} %bitcast.4, ...), custom_call_target="tpu_custom_call" | custom-call | tf_op jit(solution)/shard_map/kv_exchange/pallas_call | solution.py:533
  60.5 0.7 %kv_outputs.1 = (bf16[256,512]{1,0:T(8,128)(2,1)}, f32[24,512]{1,0:T(8,128)}, f32[1,24]{1,0:T(1,128)}) custom-call(bf16[256,512]{1,0:T(8,128)(2,1)S(1)} %get-tuple-element.9.refs_0_, f32[24,512]{1,0:T(8,128)S(1)} %get-tuple-element.10.refs_1_, f32[1,24]{1,0:T(1,128)S(1)} %get-tuple-element.11.refs_2_), custom_call_target="tpu_custom_call" | custom-call | tf_op jit(solution)/shard_map/kv_outputs/pallas_call | solution.py:578

commit v5 on v4

--- a/solution.py
+++ b/solution.py
@@ -401,15 +401,24 @@
         pl.semaphore_wait(sem_in_far, 1)
     lax.fori_loop(0, early, r2_send, 0)
     lax.fori_loop(early, jn, r1_and_r2, 0)
+    def g2_send(i):
+        at = nth(i)
+        view = full_gw.at[at, hi_own, lo_own, :, lane_tile(y)]
+        for dx, dy in peers:
+            remote(
+                piece_g.at[at], view, sem_g2s, sem_g2r.at[dx], at_plane[dx][dy]
+            ).start()
+        pltpu.make_async_copy(piece_g.at[at], view, sem_g2r.at[0]).start()
+
+    g2_send(0)
+    if jn > 1:
+        g2_send(-1)
     if jn > 2:
         ring_copy(1, nth(1), ahead).wait_recv()
+        g2_send(1)
     if jn > 3:
         ring_copy(2, nth(2), behind).wait_recv()
-
-    g2_view = full_gw.at[:, hi_own, lo_own, :, lane_tile(y)]
-    pltpu.make_async_copy(piece_g, g2_view, sem_g2r.at[0]).start()
-    for dx, dy in peers:
-        remote(piece_g, g2_view, sem_g2s, sem_g2r.at[dx], at_plane[dx][dy]).start()
+        g2_send(2)
 
     arrived(land_r0, sem_r0s)
     arrived(land_r1, sem_r1s)

time: 61.4 us -> 59.1 us (0.963)
  Pallas kernels: 60.6 us -> 58.3 us
    pallas_call x1, Pallas kernels: 59.9 us -> 57.6 us  [body(): pl.pallas_call(functools.partial(kernel, ny, nz), out_shape=shapes, in_sp...]
where the time goes in v5:
time: 59.1 us; the launch traced here: 59 us
  Pallas kernels  58.3 us (99%)
  between operations  0.64 us (1%)
    pallas_call x1, Pallas kernels, body(): pl.pallas_call(functools.partial(kernel, ny, nz), out_shape=shapes, in_sp...  57.6 us

profile of v5, /device:TPU:1, one launch (start us, length us, event | category | flops | bytes accessed | tf_op | source)
XLA Modules:
  0.0 59.0 jit_solution(14508724872359960953)
XLA Ops:
  0.6 57.6 %kv_exchange.1 = (bf16[256,512]{1,0:T(8,128)(2,1)S(1)}, f32[24,512]{1,0:T(8,128)S(1)}, f32[1,24]{1,0:T(1,128)S(1)}) custom-call(s32[16,64]{1,0:T(8,128)} %counts_hbm.1, s32[1,16]{1,0:T(1,128)} %bitcast.5, bf16[1,24]{1,0:T(2,128)(2,1)} %bitcast.6, bf16[24,512]{1,0:T(8,128)(2,1)} %weight_hbm.1, s32[2,128]{1,0:T(2,128)} %bitcast.4, ...), custom_call_target="tpu_custom_call" | custom-call | tf_op jit(solution)/shard_map/kv_exchange/pallas_call | solution.py:542
  58.2 0.7 %kv_outputs.1 = (bf16[256,512]{1,0:T(8,128)(2,1)}, f32[24,512]{1,0:T(8,128)}, f32[1,24]{1,0:T(1,128)}) custom-call(bf16[256,512]{1,0:T(8,128)(2,1)S(1)} %get-tuple-element.9.refs_0_, f32[24,512]{1,0:T(8,128)S(1)} %get-tuple-element.10.refs_1_, f32[1,24]{1,0:T(1,128)S(1)} %get-tuple-element.11.refs_2_), custom_call_target="tpu_custom_call" | custom-call | tf_op jit(solution)/shard_map/kv_outputs/pallas_call | solution.py:587

commit v6 on v5

--- a/solution.py
+++ b/solution.py
@@ -169,7 +169,7 @@
     at_other = [[(a + 1 - 2 * core, b) for a, b in line] for line in at_plane]
     sibling = at_other[0][0]
     peers = [(i, j) for i in range(4) for j in range(ny)][1:]
-    peers.sort(key=lambda p: (min(p[0], 4 - p[0]) + min(p[1], ny - p[1]), sum(p)))
+    peers.sort(key=lambda p: (-min(p[0], 4 - p[0]) - min(p[1], ny - p[1]), sum(p)))
 
     greet(sibling)
     for i, j in peers:
@@ -463,18 +463,17 @@
         back = (4 - dx) % 4
         arrived(full_gw.at[:, hi_of(xs[back], 1 - core), lo_sib], sem_g3r.at[dx])
 
-    def p_step(j, total):
-        lhs = tokens_ref[:, pl.ds(pl.multiple_of(j * group, group), group)]
-        rhs = full_gw[j].reshape(group, cols)
-        return total + jnp.dot(lhs, rhs, preferred_element_type=F32)
-
-    projected = lax.fori_loop(0, jn, p_step, jnp.zeros((rows, cols), F32))
-    projected = projected * inv_norm
-    for h in range(2 * heads):
-        part = projected[:, h * HD : (h + 1) * HD]
-        if h < heads:
-            part = part * cosines + pltpu.roll(part, HALF, 1) * sines
-        kv_ref[:, h * HD : (h + 1) * HD] = part.astype(BF16)
+    pair = 2 * LANES
+    for i in range(cols // pair):
+        rhs = full_gw[:, :, :, :, i * pair : (i + 1) * pair].reshape(width, pair)
+        projected = jnp.dot(tokens_ref[...], rhs, preferred_element_type=F32)
+        projected = projected * inv_norm
+        for h in range(pair // HD):
+            part = projected[:, h * HD : (h + 1) * HD]
+            if i * (pair // HD) + h < heads:
+                part = part * cosines + pltpu.roll(part, HALF, 1) * sines
+            at = i * pair + h * HD
+            kv_ref[:, at : at + HD] = part.astype(BF16)
 
     arrived(land_r3, sem_r3r)
     root = jnp.sqrt(live_total)

time: 59.1 us -> 59 us (level)
  no operation moved by 1% of the time
where the time goes in v6:
time: 59 us; the launch traced here: 58.9 us
  Pallas kernels  58.2 us (99%)
  between operations  0.64 us (1%)
    pallas_call x1, Pallas kernels, body(): pl.pallas_call(functools.partial(kernel, ny, nz), out_shape=shapes, in_sp...  57.5 us

profile of v6, /device:TPU:1, one launch (start us, length us, event | category | flops | bytes accessed | tf_op | source)
XLA Modules:
  0.0 58.9 jit_solution(4325965345656815757)
XLA Ops:
  0.6 57.5 %kv_exchange.1 = (bf16[256,512]{1,0:T(8,128)(2,1)S(1)}, f32[24,512]{1,0:T(8,128)S(1)}, f32[1,24]{1,0:T(1,128)S(1)}) custom-call(s32[16,64]{1,0:T(8,128)} %counts_hbm.1, s32[1,16]{1,0:T(1,128)} %bitcast.5, bf16[1,24]{1,0:T(2,128)(2,1)} %bitcast.6, bf16[24,512]{1,0:T(8,128)(2,1)} %weight_hbm.1, s32[2,128]{1,0:T(2,128)} %bitcast.4, ...), custom_call_target="tpu_custom_call" | custom-call | tf_op jit(solution)/shard_map/kv_exchange/pallas_call | solution.py:541
  58.1 0.7 %kv_outputs.1 = (bf16[256,512]{1,0:T(8,128)(2,1)}, f32[24,512]{1,0:T(8,128)}, f32[1,24]{1,0:T(1,128)}) custom-call(bf16[256,512]{1,0:T(8,128)(2,1)S(1)} %get-tuple-element.9.refs_0_, f32[24,512]{1,0:T(8,128)S(1)} %get-tuple-element.10.refs_1_, f32[1,24]{1,0:T(1,128)S(1)} %get-tuple-element.11.refs_2_), custom_call_target="tpu_custom_call" | custom-call | tf_op jit(solution)/shard_map/kv_outputs/pallas_call | solution.py:586
